TPU v7x, 32 devices: a whole 2x2x4 slice. The times are simulated.
32 devices in a mesh: groups: 2 (over x), wide: 8 (over z, y), narrow: 2 (over core).
Axes of the slice: x: 2, y: 2, z: 4, core: 2. Of those that a mesh axis runs over, the one named last changes fastest.
Arguments:
- context_symbol_ids: int32 [2, 16, 16], P('narrow', 'groups'), parts along dimension 1, may hold values from 0 to 32767
- context_symbol_spans: int32 [2, 16], P('narrow', 'groups'), parts along dimension 1, may hold values from 1 to 16, as said below
- symbol_vector_lookup: bfloat16 [4096, 32768], P('wide'), may hold values from -6 to 6
- opening_lagged_blend: float32 [4096], replicated, may hold values from 0 to 1
- lagged_blend_weights: float32 [3, 4096], replicated, may hold values from 0 to 1
- blending_left_operand: bfloat16 [4096, 192], replicated, may hold values from -0.09375 to 0.09375
- blending_right_operands: bfloat16 [3, 64, 4096], replicated, may hold values from -0.375 to 0.375
- fixed_fading_scores: float32 [4096], P('wide'), may hold values from -6 to -1
- fading_left_operand: bfloat16 [4096, 128], replicated, may hold values from -0.09375 to 0.09375
- fading_right_operand: bfloat16 [128, 4096], P(None, 'wide'), may hold values from -0.5 to 0.5
- address_projector: bfloat16 [4096, 4096], P('wide'), may hold values from -0.09375 to 0.09375
- payload_projector: bfloat16 [4096, 4096], P('wide'), may hold values from -0.09375 to 0.09375
- present_symbol_reward: float32 [64, 64], replicated, may hold values from -1 to 1
- cluster_scaling_weight: float32 [4096], replicated, may hold values from 0.5 to 1.5
- cluster_scaling_offset: float32 [4096], replicated, may hold values from -3 to 3
- generated_acceptance: bfloat16 [2, 16, 4, 4096], P(None, ('groups', 'wide'), None, 'narrow'), parts along dimension 1, may hold values from -6 to 6
- generated_addresses: bfloat16 [2, 16, 4, 4096], P(None, ('groups', 'wide'), None, 'narrow'), parts along dimension 1, may hold values from -6 to 6
- generated_payloads: bfloat16 [2, 16, 4, 4096], P(None, ('groups', 'wide'), None, 'narrow'), parts along dimension 1, may hold values from -6 to 6
- generated_fading_scores: bfloat16 [2, 16, 4, 4096], P(None, ('groups', 'wide'), None, 'narrow'), parts along dimension 1, may hold values from -6 to -1
- generated_valve_scores: bfloat16 [2, 16, 4, 4096], P(None, ('groups', 'wide'), None, 'narrow'), parts along dimension 1, may hold values from -6 to 6
Outputs:
- dec_out: bfloat16 [2, 16, 4, 4096], P(None, ('groups', 'wide'), None, 'narrow'), parts along dimension 1
There are 2 independent parts, one for each index of `groups`. A program takes and returns all parts, laid end to end along the dimension named above; an argument that names none is the same for every part. Nothing has to cross between parts.
Inputs may be any that keep to these rules, and one draw needn't show every extreme that they name: `context_symbol_spans`: positions at or past a prompt's length are padding. In every draw one of the 2 banks, chosen by the draw, holds only prompts of exactly 16 tokens, and every other bank holds at least one prompt of 16 tokens.
All inputs are finite; a program needn't handle non-finite values.
Results may differ from a plain program's by a relative error of at most 0.0095.
Values may be sent and summed in bfloat16 or wider, within the bound.
No kernel may reach another device: no remote copies, remote signals or barrier semaphores. Data moves between devices by JAX's collectives and lax.ppermute only.
A program may use at most 128 MiB of HBM per device.

v0:
```python
import jax
import jax.numpy as jnp
from jax import lax
from jax.sharding import PartitionSpec as P

norm_eps = 0.00064


def mix_project(
    embedded,
    opening_lagged_blend,
    lagged_blend_weights,
    blending_left_operand,
    blending_right_operands,
    fixed_fading_scores,
    fading_left_operand,
    fading_right_operand,
    address_projector,
    payload_projector,
):
    features = embedded.shape[2]
    previous = jnp.pad(embedded, ((0, 0), (1, 0), (0, 0)))[:, :-1, :]
    current = embedded.reshape(-1, features).astype(jnp.float32)
    difference = previous.reshape(-1, features).astype(jnp.float32) - current
    mixed_in = (current + difference * opening_lagged_blend).astype(jnp.bfloat16)
    hidden = jnp.tanh(
        jnp.dot(mixed_in, blending_left_operand, preferred_element_type=jnp.float32)
    ).astype(jnp.bfloat16)
    rank_size = blending_right_operands.shape[1]
    branches = []
    for branch in range(3):
        shift_term = jnp.dot(
            hidden[:, branch * rank_size : (branch + 1) * rank_size],
            blending_right_operands[branch],
            preferred_element_type=jnp.float32,
        )
        branches.append(
            (current + difference * (lagged_blend_weights[branch] + shift_term)).astype(
                jnp.bfloat16
            )
        )
    decay_hidden = jnp.tanh(
        jnp.dot(branches[0], fading_left_operand, preferred_element_type=jnp.float32)
    ).astype(jnp.bfloat16)
    decay_log = fixed_fading_scores + jnp.dot(
        decay_hidden, fading_right_operand, preferred_element_type=jnp.float32
    )
    key_proj = jnp.dot(branches[1], address_projector.T, preferred_element_type=jnp.float32).astype(
        jnp.bfloat16
    )
    value_proj = jnp.dot(
        branches[2], payload_projector.T, preferred_element_type=jnp.float32
    ).astype(jnp.bfloat16)
    return (key_proj, value_proj, decay_log)


def final_states(key_proj, value_proj, decay_log, lengths, attender_width):
    bank_rows, length, columns = key_proj.shape
    attender_ordinal = columns // attender_width
    decay_rates = jnp.exp(decay_log)
    places = lax.broadcasted_iota(jnp.int32, (bank_rows, length), 1)
    live_mask = (places < lengths[:, None])[:, :, None]
    running = jnp.cumsum(jnp.where(live_mask, decay_rates, 0.0), axis=1)
    remaining = running[:, -1:, :] - running
    weights = jnp.where(live_mask, jnp.exp(-remaining), 0.0)
    weighted = (key_proj.astype(jnp.float32) * weights).reshape(
        bank_rows, length, attender_ordinal, attender_width
    )
    plain_values = value_proj.astype(jnp.float32).reshape(
        bank_rows, length, attender_ordinal, attender_width
    )
    return jnp.einsum("rlhi,rlhj->rhij", weighted, plain_values, precision=lax.Precision.HIGHEST)


def generation_iterations(
    recurrent_memories,
    acceptance_lines,
    address_source,
    payload_source,
    fading_source,
    valve_source,
    shard_reward,
    shard_scaling_weight,
    shard_scaling_offset,
):
    attender_ordinal = recurrent_memories.shape[-3]
    attender_width = recurrent_memories.shape[-1]
    leading = acceptance_lines.shape[:-2]
    step_count = acceptance_lines.shape[-2]
    split_shape = leading + (step_count, attender_ordinal, attender_width)
    receptance = acceptance_lines.astype(jnp.float32).reshape(split_shape)
    key_split = address_source.astype(jnp.float32).reshape(split_shape)
    valued = payload_source.astype(jnp.float32).reshape(split_shape)
    factors = jnp.exp(-jnp.exp(fading_source.astype(jnp.float32))).reshape(split_shape)
    results = []
    for position in range(step_count):
        present_acceptance = receptance[..., position, :, :]
        present_address = key_split[..., position, :, :]
        present_payload = valued[..., position, :, :]
        immediate_summand = (
            jnp.sum(present_acceptance * shard_reward * present_address, axis=-1, keepdims=True)
            * present_payload
        )
        carried = jnp.einsum(
            "...hi,...hij->...hj",
            present_acceptance,
            recurrent_memories,
            precision=lax.Precision.HIGHEST,
        )
        results.append(carried + immediate_summand)
        if position + 1 < step_count:
            recurrent_memories = (
                factors[..., position, :, :][..., :, None] * recurrent_memories
                + present_address[..., :, None] * present_payload[..., None, :]
            )
    mixed_out = jnp.stack(results, axis=-3)
    average = jnp.mean(mixed_out, axis=-1, keepdims=True)
    centred = mixed_out - average
    spread = jnp.mean(centred * centred, axis=-1, keepdims=True)
    normed = (centred * lax.rsqrt(spread + norm_eps)).reshape(
        leading + (step_count, attender_ordinal * attender_width)
    )
    return (
        (normed * shard_scaling_weight + shard_scaling_offset)
        * jax.nn.silu(valve_source.astype(jnp.float32))
    ).astype(jnp.bfloat16)


def per_device(
    context_symbol_ids,
    context_symbol_spans,
    symbol_vector_lookup,
    opening_lagged_blend,
    lagged_blend_weights,
    blending_left_operand,
    blending_right_operands,
    fixed_fading_scores,
    fading_left_operand,
    fading_right_operand,
    address_projector,
    payload_projector,
    present_symbol_reward,
    cluster_scaling_weight,
    cluster_scaling_offset,
    generated_acceptance,
    generated_addresses,
    generated_payloads,
    generated_fading_scores,
    generated_valve_scores,
):
    bank_rows = context_symbol_ids.shape[1]
    length = context_symbol_ids.shape[2]
    columns = symbol_vector_lookup.shape[0]
    attender_width = present_symbol_reward.shape[1]
    head_local = columns // attender_width
    lengths = context_symbol_spans.reshape(-1)
    picked = jnp.take(symbol_vector_lookup, context_symbol_ids.reshape(-1), axis=1)
    gathered = lax.all_gather(picked, "wide", axis=0, tiled=True).T
    features = gathered.shape[1]
    block_rows = bank_rows
    while block_rows % 2 == 0 and block_rows * length > 1024:
        block_rows = block_rows // 2
    blocks = gathered.reshape(bank_rows // block_rows, block_rows, length, features)
    length_blocks = lengths.reshape(bank_rows // block_rows, block_rows)

    def one_block(block_item):
        key_proj, value_proj, decay_log = mix_project(
            block_item[0],
            opening_lagged_blend,
            lagged_blend_weights,
            blending_left_operand,
            blending_right_operands,
            fixed_fading_scores,
            fading_left_operand,
            fading_right_operand,
            address_projector,
            payload_projector,
        )
        block_shape = (block_rows, length, columns)
        return final_states(
            key_proj.reshape(block_shape),
            value_proj.reshape(block_shape),
            decay_log.reshape(block_shape),
            block_item[1],
            attender_width,
        )

    recurrent_memories = lax.map(one_block, (blocks, length_blocks)).reshape(
        bank_rows, head_local, attender_width, attender_width
    )
    handed = lax.all_to_all(
        lax.all_to_all(
            recurrent_memories.reshape(1, bank_rows, head_local, attender_width * attender_width),
            "wide",
            split_axis=1,
            concat_axis=2,
            tiled=True,
        ),
        "narrow",
        split_axis=2,
        concat_axis=0,
        tiled=True,
    )
    generated_by_attender = handed.shape[2]
    leading_attender_offset = lax.axis_index("narrow") * generated_by_attender
    shard_reward = lax.dynamic_slice_in_dim(
        present_symbol_reward, leading_attender_offset, generated_by_attender, 0
    )
    shard_scaling_weight = lax.dynamic_slice_in_dim(
        cluster_scaling_weight,
        leading_attender_offset * attender_width,
        generated_by_attender * attender_width,
        0,
    )
    shard_scaling_offset = lax.dynamic_slice_in_dim(
        cluster_scaling_offset,
        leading_attender_offset * attender_width,
        generated_by_attender * attender_width,
        0,
    )
    result = generation_iterations(
        handed.reshape(handed.shape[:3] + (attender_width, attender_width)),
        generated_acceptance,
        generated_addresses,
        generated_payloads,
        generated_fading_scores,
        generated_valve_scores,
        shard_reward,
        shard_scaling_weight,
        shard_scaling_offset,
    )
    return result


def solution(mesh):
    placed = (
        P("narrow", "groups", None),
        P("narrow", "groups"),
        P("wide", None),
        P(),
        P(),
        P(),
        P(),
        P("wide"),
        P(),
        P(None, "wide"),
        P("wide", None),
        P("wide", None),
        P(),
        P(),
        P(),
        P(None, ("groups", "wide"), None, "narrow"),
        P(None, ("groups", "wide"), None, "narrow"),
        P(None, ("groups", "wide"), None, "narrow"),
        P(None, ("groups", "wide"), None, "narrow"),
        P(None, ("groups", "wide"), None, "narrow"),
    )
    return jax.shard_map(
        per_device,
        mesh=mesh,
        in_specs=placed,
        out_specs=P(None, ("groups", "wide"), None, "narrow"),
        check_vma=False,
    )
```

profile of v0, /device:TPU:0, one launch (start us, length us, event | category | flops | bytes accessed | tf_op | source)
XLA Modules:
  0.0 180.6 jit_solution(2919527989202924769)
XLA Ops:
  6.5 0.9 reshape.534
  7.4 0.8 reshape.533
  8.2 44.0 %copy.70 = bf16[512,32768]{0,1:T(8,128)(2,1)} copy(bf16[512,32768]{1,0:T(8,128)(2,1)} %param.22) | data formatting | bytes 67108864 | tf_op args[2]
  52.2 2.0 %gather_fusion = bf16[128,512]{1,0:T(8,128)(2,1)S(1)} fusion(bf16[512,32768]{0,1:T(8,128)(2,1)} %copy.70, s32[1024]{0:T(1024)S(1)} %pad_clamp_fusion), kind=kCustom, calls=%fused_computation | custom fusion | bytes 262656 | tf_op jit(solution)/shard_map/jit(_take)/gather | solution.py:157
  54.2 0.7 select_bitcast_fusion
  55.0 0.1 copy.71
  55.1 42.1 %all-gather.2.cloned.1.call-done = bf16[4096,128]{0,1:T(8,128)(2,1)} async-done(((bf16[512,128]{0,1:T(8,128)(2,1)}), bf16[4096,128]{0,1:T(8,128)(2,1)}) %all-gather.2.cloned.1.call-update) | async-done | bytes 1048592 | tf_op jit(solution)/shard_map/all_gather | solution.py:158
  97.2 1.6 pad_slice_fusion
  98.8 0.7 fusion.20
  99.5 0.3 copy-done.4
  99.8 2.7 %fusion.22 = bf16[128,128]{1,0:T(8,128)(2,1)S(1)} fusion(bf16[4096,128]{1,0:T(8,128)(2,1)} %param.28, bf16[128,4096]{1,0:T(8,128)(2,1)} %bitcast.181, bf16[4096,128]{0,1:T(8,128)(2,1)S(1)} %copy-done.3, f32[4096]{0:T(1024)S(1)} %bitcast.199, bf16[3,64,4096]{2,1,0:T(8,128)(2,1)} %param.26, bf16[128,192]{0,1:T(8,128)(2,1)S(1)} %fusion.20), kind=kOutput, calls=%fused_computation.35 | convolution fusion | flops 205012992 | bytes 3735552 | tf_op jit(solution)/shard_map/while/body/eval_jaxpr/dot_general | solution.py:43
  102.6 0.2 fusion.18
  102.7 0.2 fusion.68
  102.9 0.1 reduce_window_sum.15
  103.1 0.1 sub.51
  103.2 4.7 %convolution_convert_fusion = bf16[128,512]{1,0:T(8,128)(2,1)S(1)} fusion(bf16[512,4096]{1,0:T(8,128)(2,1)} %param.31, bf16[128,4096]{1,0:T(8,128)(2,1)} %bitcast.182, bf16[4096,128]{0,1:T(8,128)(2,1)S(1)} %copy-done.3, f32[4096]{0:T(1024)S(1)} %bitcast.198, bf16[3,64,4096]{2,1,0:T(8,128)(2,1)} %param.26, bf16[128,192]{0,1:T(8,128)(2,1)S(1)} %fusion.20), kind=kOutput, calls=%fused_computation.29 | convolution fusion | flops 607715328 | bytes 6979584 | tf_op jit(solution)/shard_map/while/body/eval_jaxpr/dot_general | solution.py:51
  107.8 0.2 reshape.535
  108.0 4.7 %fusion.19 = f32[128,512]{1,0:T(8,128)S(1)} fusion(bf16[512,4096]{1,0:T(8,128)(2,1)} %param.30, bf16[128,4096]{1,0:T(8,128)(2,1)} %bitcast.183, bf16[4096,128]{0,1:T(8,128)(2,1)S(1)} %copy-done.3, f32[4096]{0:T(1024)S(1)} %bitcast.197, bf16[3,64,4096]{2,1,0:T(8,128)(2,1)} %param.26, bf16[128,192]{0,1:T(8,128)(2,1)S(1)} %fusion.20), kind=kOutput, calls=%fused_computation.31 | convolution fusion | flops 607780864 | bytes 7110656 | tf_op jit(solution)/shard_map/while/body/eval_jaxpr/dot_general | solution.py:48
  112.7 0.1 reshape.549
  112.8 3.3 %fusion.56 = f32[8,8,64,64]{3,2,1,0:T(8,128)} fusion(f32[8,16,8,64]{3,2,1,0:T(8,128)S(1)} %reshape.549, f32[8,16,8,64]{3,2,0,1:T(8,128)S(1)} %reduce_window_sum.15, bf16[8,16,8,64]{3,2,1,0:T(8,128)(2,1)S(1)} %reshape.535, f32[8,8,64]{2,1,0:T(8,128)S(1)} %sub.51, pred[8,16]{1,0:T(8,128)(4,1)S(1)} %copy.71), kind=kOutput, calls=%fused_computation.66 | convolution fusion | flops 50593792 | bytes 1720448 | tf_op jit(solution)/shard_map/while/body/eval_jaxpr/rlhi,rlhj->rhij/dot_general | solution.py:72
  116.1 2.9 %reshape_reshape.3 = f32[1,8,8,4096]{3,2,1,0:T(8,128)} reshape(f32[8,8,64,64]{3,2,1,0:T(8,128)} %fusion.56) | data formatting | bytes 2097152 | tf_op jit(solution)/shard_map/reshape;reshape | solution.py:193
  119.1 3.8 %all-to-all-start = ((f32[1,8,8,4096]{3,2,0,1:T(8,128)}), f32[1,8,8,4096]{3,2,0,1:T(8,128)S(1)}, u32[]{:S(2)}, u32[]{:S(2)}) async-start(f32[1,8,8,4096]{3,2,0,1:T(8,128)} %bitcast.13), calls=%async_computation | async-start | bytes 2097152 | tf_op jit(solution)/shard_map/all_to_all | solution.py:192
  122.8 0.1 reshape.553
  123.0 0.1 reshape.544
  123.1 0.1 reshape.551
  123.2 0.1 reshape.537
  123.4 0.1 fusion.95
  123.6 23.9 %all-to-all-done = f32[1,8,8,4096]{3,2,0,1:T(8,128)S(1)} async-done(((f32[1,8,8,4096]{3,2,0,1:T(8,128)}), f32[1,8,8,4096]{3,2,0,1:T(8,128)S(1)}, u32[]{:S(2)}, u32[]{:S(2)}) %all-to-all-start) | async-done | bytes 1048608 | tf_op jit(solution)/shard_map/all_to_all | solution.py:192
  147.5 1.1 copy.77
  148.6 4.6 %all_to_all.21 = f32[1,1,64,4096]{3,1,0,2:T(1,128)S(1)} all-to-all(f32[1,1,64,4096]{3,1,0,2:T(1,128)S(1)} %copy.77), channel_id=1, replica_groups=mesh['groups'=2,'wide'=8,'narrow'=2] {'narrow'}, dimensions={2} | all-to-all | bytes 2097152 | tf_op jit(solution)/shard_map/all_to_all | solution.py:191
  153.1 2.6 %reduce.6 = f32[64,4096]{1,0:T(8,128)S(1)} reduce(f32[1,1,64,4096]{3,1,0,2:T(1,128)S(1)} %all_to_all.21, f32[]{:T(128)} %constant.68), dimensions={0,1}, to_apply=%all_to_all.8.reduce_sub_computation | reduce | bytes 2097156 | tf_op jit(solution)/shard_map/all_to_all | solution.py:191
  155.8 2.2 %reshape.536 = f32[2,32,64,64]{3,2,1,0:T(8,128)} reshape(f32[64,4096]{1,0:T(8,128)S(1)} %reduce.6) | data formatting | bytes 2097152 | tf_op jit(solution)/shard_map/reshape.34
  158.0 2.8 %fusion.99 = f32[2,32,1,64]{3,2,1,0:T(1,128)S(1)} fusion(f32[2,32,64,64]{3,2,1,0:T(8,128)} %reshape.536, bf16[2,32,64,1]{2,1,0,3:T(8,128)(2,1)S(1)} %get-tuple-element.61), kind=kOutput, calls=%fused_computation.127 | convolution fusion | flops 3145728 | bytes 1073152 | tf_op jit(solution)/shard_map/...hi,...hij->...hj/dot_general | solution.py:104
  160.8 2.0 %fusion.15 = f32[2,32,1,64]{3,2,1,0:T(1,128)S(1)} fusion(f32[2,32,64,64]{3,2,1,0:T(8,128)S(1)} %copy-done.2, f32[2,32,64]{2,1,0:T(8,128)S(1)} %get-tuple-element.70, f32[2,32,64]{2,1,0:T(8,128)S(1)} %get-tuple-element.54, f32[2,32,64]{2,1,0:T(8,128)S(1)} %get-tuple-element.37, bf16[2,32,64,1]{2,1,0,3:T(8,128)(2,1)S(1)} %get-tuple-element.64), kind=kOutput, calls=%fused_computation.23 | convolution fusion | flops 3932160 | bytes 1122304 | tf_op jit(solution)/shard_map/...hi,...hij->...hj/dot_general | solution.py:104
  162.8 3.5 %fusion.17 = f32[2,32,1,64]{3,2,1,0:T(1,128)S(1)} fusion(f32[2,32,64,64]{3,2,1,0:T(8,128)S(1)} %copy-done.2, f32[2,32,64]{2,1,0:T(8,128)S(1)} %get-tuple-element.68, f32[2,32,64]{2,1,0:T(8,128)S(1)} %get-tuple-element.56, f32[2,32,64]{2,1,0:T(8,128)S(1)} %get-tuple-element.52, f32[2,32,64]{2,1,0:T(8,128)S(1)} %get-tuple-element.70, ...), kind=kOutput, calls=%fused_computation.26 | convolution fusion | flops 4718592 | bytes 1171456 | tf_op jit(solution)/shard_map/...hi,...hij->...hj/dot_general | solution.py:104
  166.3 5.3 %fusion.11 = f32[2,32,1,64]{3,2,1,0:T(1,128)S(1)} fusion(f32[2,32,64,64]{3,2,1,0:T(8,128)S(1)} %copy-done.2, f32[2,32,64]{2,1,0:T(8,128)S(1)} %get-tuple-element.69, f32[2,32,64]{2,1,0:T(8,128)S(1)} %get-tuple-element.57, f32[2,32,64]{2,1,0:T(8,128)S(1)} %get-tuple-element.38, f32[2,32,64]{2,1,0:T(8,128)S(1)} %get-tuple-element.68, ...), kind=kOutput, calls=%fused_computation.17 | convolution fusion | flops 5505024 | bytes 1220608 | tf_op jit(solution)/shard_map/...hi,...hij->...hj/dot_general | solution.py:104
  171.7 0.1 multiply_add_fusion.7
  171.8 0.1 fusion.74
  171.9 0.2 multiply_reduce_fusion
  172.1 0.1 stack.35
  172.2 0.1 stack.36
  172.3 0.1 stack.37
  172.4 0.1 stack.38
  172.5 0.1 mul.379
  172.6 0.1 mul.380
  172.7 0.1 sub.54
  172.8 0.1 sub.55
  173.0 0.7 fusion.81
  (53 shorter events, 0.3 us)
Async XLA Ops:
  6.5 92.3 %copy-start = (bf16[4096,192]{0,1:T(8,128)(2,1)S(1)}, bf16[4096,192]{0,1:T(8,128)(2,1)}, u32[]{:S(2)}) copy-start(bf16[4096,192]{0,1:T(8,128)(2,1)} %param.25) | copy-start | bytes 4718596
  6.5 90.7 %all-gather.2.cloned.1.call-start = ((), (), s32[]{:S(2)}) async-start(), calls=%async_computation.2 | async-start | bytes 1179648 | tf_op jit(solution)/shard_map/all_gather | solution.py:158
  8.2 46.8 %copy-start.14 = (s32[1,8]{1,0:T(1,128)S(1)}, s32[1,8]{1,0:T(1,128)}, u32[]{:S(2)}) copy-start(s32[1,8]{1,0:T(1,128)} %param.21) | copy-start | bytes 100
  8.2 46.9 %copy-start.6 = (f32[3,4096]{1,0:T(4,128)S(1)}, f32[3,4096]{1,0:T(4,128)}, u32[]{:S(2)}) copy-start(f32[3,4096]{1,0:T(4,128)} %param.24) | copy-start | bytes 147460
  52.2 46.6 %copy-start.15 = (f32[4096]{0:T(1024)S(1)}, f32[4096]{0:T(1024)}, u32[]{:S(2)}) copy-start(f32[4096]{0:T(1024)} %param.23) | copy-start | bytes 49156
  97.2 1.6 copy-start.3
  98.8 1.0 copy-start.4
  99.8 2.7 %copy-start.5 = (bf16[128,512]{1,0:T(8,128)(2,1)S(1)}, bf16[128,512]{1,0:T(8,128)(2,1)}, u32[]{:S(2)}) copy-start(bf16[128,512]{1,0:T(8,128)(2,1)} %param.29) | copy-start | bytes 393220
  99.8 2.7 %copy-start.13 = (f32[512]{0:T(512)S(1)}, f32[512]{0:T(512)}, u32[]{:S(2)}) copy-start(f32[512]{0:T(512)} %param.27) | copy-start | bytes 6148
  116.1 6.7 %copy-start.7 = (bf16[2,1,4,2048]{3,2,1,0:T(4,128)(2,1)S(1)}, bf16[2,1,4,2048]{3,2,1,0:T(4,128)(2,1)}, u32[]{:S(2)}) copy-start(bf16[2,1,4,2048]{3,2,1,0:T(4,128)(2,1)} %param.37) | copy-start | bytes 98308
  116.1 6.8 %copy-start.8 = (bf16[2,1,4,2048]{3,2,1,0:T(4,128)(2,1)S(1)}, bf16[2,1,4,2048]{3,2,1,0:T(4,128)(2,1)}, u32[]{:S(2)}) copy-start(bf16[2,1,4,2048]{3,2,1,0:T(4,128)(2,1)} %param.38) | copy-start | bytes 98308
  116.1 7.0 %copy-start.9 = (bf16[2,1,4,2048]{3,2,1,0:T(4,128)(2,1)S(1)}, bf16[2,1,4,2048]{3,2,1,0:T(4,128)(2,1)}, u32[]{:S(2)}) copy-start(bf16[2,1,4,2048]{3,2,1,0:T(4,128)(2,1)} %param.36) | copy-start | bytes 98308
  119.1 4.2 %copy-start.10 = (bf16[2,1,4,2048]{3,2,1,0:T(4,128)(2,1)S(1)}, bf16[2,1,4,2048]{3,2,1,0:T(4,128)(2,1)}, u32[]{:S(2)}) copy-start(bf16[2,1,4,2048]{3,2,1,0:T(4,128)(2,1)} %param.35) | copy-start | bytes 98308
  119.1 4.3 %copy-start.12 = (f32[64,64]{1,0:T(8,128)S(1)}, f32[64,64]{1,0:T(8,128)}, u32[]{:S(2)}) copy-start(f32[64,64]{1,0:T(8,128)} %param.32) | copy-start | bytes 49156
  119.1 28.4 %all-to-all-start = ((f32[1,8,8,4096]{3,2,0,1:T(8,128)}), f32[1,8,8,4096]{3,2,0,1:T(8,128)S(1)}, u32[]{:S(2)}, u32[]{:S(2)}) async-start(f32[1,8,8,4096]{3,2,0,1:T(8,128)} %bitcast.13), calls=%async_computation | async-start | bytes 2097152 | tf_op jit(solution)/shard_map/all_to_all | solution.py:192
  158.0 2.8 %copy-start.2 = (f32[2,32,64,64]{3,2,1,0:T(8,128)S(1)}, f32[2,32,64,64]{3,2,1,0:T(8,128)}, u32[]{:S(2)}) copy-start(f32[2,32,64,64]{3,2,1,0:T(8,128)} %reshape.536) | copy-start | bytes 3145732
  166.3 6.7 %copy-start.11 = (bf16[2,1,4,2048]{3,2,1,0:T(4,128)(2,1)S(1)}, bf16[2,1,4,2048]{3,2,1,0:T(4,128)(2,1)}, u32[]{:S(2)}) copy-start(bf16[2,1,4,2048]{3,2,1,0:T(4,128)(2,1)} %param.39) | copy-start | bytes 98308
  166.3 6.7 %dynamic-slice-start = ((f32[4096]{0:T(1024)}, s32[]{:T(128)}), f32[2048]{0:T(1024)S(1)}, s32[]{:S(2)}) async-start(f32[4096]{0:T(1024)} %param.33, s32[]{:T(128)} %select_n.43), calls=%async_computation.3 | async-start | bytes 16896 | tf_op jit(solution)/shard_map/dynamic_slice | solution.py:209
  166.3 6.6 %dynamic-slice-start.1 = ((f32[4096]{0:T(1024)}, s32[]{:T(128)}), f32[2048]{0:T(1024)S(1)}, s32[]{:S(2)}) async-start(f32[4096]{0:T(1024)} %param.34, s32[]{:T(128)} %select_n.43), calls=%async_computation.4 | async-start | bytes 16896 | tf_op jit(solution)/shard_map/dynamic_slice | solution.py:215
  166.3 7.4 %copy-start.1 = (bf16[4096,192]{0,1:T(8,128)(2,1)S(1)}, bf16[4096,192]{0,1:T(8,128)(2,1)}, u32[]{:S(2)}) copy-start(bf16[4096,192]{0,1:T(8,128)(2,1)} %param.25) | copy-start | bytes 4718596
Sparse Core Ops, SparseCore 0:
  55.1 42.1 all-gather.1
where the time goes:
time: 182 us; the launch traced here: 181 us
  waiting for transfers between devices  66 us (36%)
  local copies, waits for them, and re-layouts  57.7 us (32%)
  matrix products  29.8 us (16%)
  between operations  13.8 us (8%)
  other arithmetic  4.89 us (3%)
  blocking collectives  4.58 us (3%)
  starting transfers between devices  3.77 us (2%)
    unnamed x33, local copies, waits for them, and re-layouts  44.4 us
    all_gather x1, waiting for transfers between devices, per_device(): gathered = lax.all_gather(picked, 'wide', axis=0, tiled=True).T  42.1 us
    all_to_all x1, waiting for transfers between devices, per_device(): lax.all_to_all(recurrent_memories.reshape(1, bank_rows, head_local, atten...  23.9 us
    dot_general x4, matrix products, generation_iterations(): jnp.einsum('...hi,...hij->...hj', present_acceptance, recurrent_memories,...  13.7 us
    dot_general x1, matrix products, mix_project(): jnp.dot(branches[1], address_projector.T, preferred_element_type=jnp.floa...  4.66 us
    dot_general x1, matrix products, mix_project(): jnp.dot(branches[2], payload_projector.T, preferred_element_type=jnp.floa...  4.65 us
    all_to_all x1, blocking collectives, per_device(): lax.all_to_all(lax.all_to_all(recurrent_memories.reshape(1, bank_rows, he...  4.58 us
    all_to_all x1, starting transfers between devices, per_device(): lax.all_to_all(recurrent_memories.reshape(1, bank_rows, head_local, atten...  3.77 us
  transfers between devices with their start and end apart: 2, of which 2 were waited for; matrix products, arithmetic and copies ran while one was open for 0% of the time, Pallas kernels for 0%

commit v1 on v0

v1 whole, which is shorter than its diff:
```python
import functools

import jax
import jax.numpy as jnp
from jax import lax
from jax.experimental import pallas as pl
from jax.experimental.pallas import tpu as pltpu
from jax.sharding import PartitionSpec as P

norm_eps = 0.00064
LANES = 128
bf16 = jnp.bfloat16
f32 = jnp.float32
NT = (((1,), (1,)), ((), ()))
VMEM = pl.BlockSpec(memory_space=pltpu.VMEM)
SMEM = pl.BlockSpec(memory_space=pltpu.SMEM)
ANY = pl.BlockSpec(memory_space=pl.ANY)


def dot(a, b):
    return jnp.dot(a, b, preferred_element_type=f32)


def dot_nt(a, b):
    return lax.dot_general(a, b, NT, preferred_element_type=f32)


def bf16_parts(x, count):
    parts = []
    for _ in range(count - 1):
        head = x.astype(bf16)
        parts.append(head)
        x = x - head.astype(f32)
    parts.append(x.astype(bf16))
    return parts


def pick_kernel(ids_ref, table_ref, out_ref, held, placed, sems, *, batch):
    tokens = held.shape[0]
    features = held.shape[1]
    batches = tokens // batch

    def copy(token):
        block = ids_ref[token] // LANES
        return pltpu.make_async_copy(
            table_ref.at[:, pl.ds(pl.multiple_of(block * LANES, LANES), LANES)],
            held.at[token],
            sems.at[token // batch],
        )

    def start(token, carry):
        copy(token).start()
        return carry

    lax.fori_loop(0, tokens, start, 0)
    rows = min(features, 64)
    lane = lax.broadcasted_iota(jnp.int32, (rows, LANES), 1)

    for group in range(batches):
        first = group * batch
        def wait(token, carry, first=first):
            copy(first + token).wait()
            return carry

        lax.fori_loop(0, batch, wait, 0)
        slot = first // LANES
        shifts = [
            jnp.remainder(first % LANES + k - ids_ref[first + k], LANES) for k in range(batch)
        ]

        def strip(step, carry, first=first, slot=slot, shifts=shifts):
            here = pl.ds(pl.multiple_of(step * rows, rows), rows)
            total = placed[slot, here, :]
            for k in range(batch):
                moved = pltpu.roll(held[first + k, here, :].astype(f32), shifts[k], 1)
                total = jnp.where(lane == first % LANES + k, moved, total)
            placed[slot, here, :] = total
            return carry

        lax.fori_loop(0, features // rows, strip, 0)
    for slot in range(placed.shape[0]):
        out_ref[slot * LANES : (slot + 1) * LANES, :] = placed[slot].T.astype(bf16)


def pick(table, ids):
    features = table.shape[0]
    tokens = ids.shape[0]
    batch = 16
    return pl.pallas_call(
        functools.partial(pick_kernel, batch=batch),
        out_shape=jax.ShapeDtypeStruct((tokens, features), bf16),
        in_specs=[SMEM, ANY],
        out_specs=VMEM,
        scratch_shapes=[
            pltpu.VMEM((tokens, features, LANES), bf16),
            pltpu.VMEM((tokens // LANES, features, LANES), f32),
            pltpu.SemaphoreType.DMA((tokens // batch,)),
        ],
        cost_estimate=pl.CostEstimate(
            flops=0, bytes_accessed=tokens * features * LANES * 2, transcendentals=0
        ),
        name="pick",
    )(ids, table)


def factor_kernel(
    owners_ref,
    spans_ref,
    *refs,
    blocks,
    width,
    length,
    rank,
):
    embeds = refs[:blocks]
    (
        opening_ref,
        lagged_ref,
        left_ref,
        right_ref,
        fixed_ref,
        decay_left_ref,
        decay_right_ref,
        key_ref,
        value_ref,
        out_ref,
        gap_ref,
    ) = refs[blocks:]
    rows = embeds[0].shape[0]
    places = lax.broadcasted_iota(jnp.int32, (rows, width), 0) % length
    first = places == 0
    strips = embeds[0].shape[1] // width

    def spots():
        for block in range(blocks):
            base = owners_ref[block] * embeds[block].shape[1]
            for strip in range(strips):
                column = base + strip * width
                where = pl.ds(pl.multiple_of(column, width), width)
                yield block * strips + strip, embeds[block], slice(strip * width, (strip + 1) * width), where

    hidden = None
    for index, ref, here, there in spots():
        current = ref[:, here].astype(f32)
        gap = jnp.where(first, 0.0, pltpu.roll(current, 1, 0)) - current
        gap_ref[:, index * width : (index + 1) * width] = gap
        mixed = (current + gap * opening_ref[:, there]).astype(bf16)
        part = dot_nt(mixed, left_ref[:, there])
        hidden = part if hidden is None else hidden + part
    hidden = jnp.tanh(hidden).astype(bf16)
    lows = [hidden[:, j * rank : (j + 1) * rank] for j in range(3)]
    sums = [None, None, None]
    for index, ref, here, there in spots():
        current = ref[:, here].astype(f32)
        gap = gap_ref[:, index * width : (index + 1) * width]
        for j in range(3):
            shift = lagged_ref[j : j + 1, there] + dot(lows[j], right_ref[j, :, there])
            branch = (current + gap * shift).astype(bf16)
            if j == 0:
                part = dot(branch, decay_left_ref[there, :])
            else:
                part = dot_nt(branch, (key_ref, value_ref)[j - 1][:, there])
            sums[j] = part if sums[j] is None else sums[j] + part
    decay_hidden = jnp.tanh(sums[0]).astype(bf16)
    decay_log = fixed_ref[...] + dot(decay_hidden, decay_right_ref[...])
    keys = sums[1].astype(bf16).astype(f32)
    values = sums[2].astype(bf16)
    rates = jnp.exp(decay_log)
    shape = (rows, rows)
    row = lax.broadcasted_iota(jnp.int32, shape, 0)
    column = lax.broadcasted_iota(jnp.int32, shape, 1)
    prompts = rows // length
    base = pl.program_id(0) * prompts
    span_of = jnp.zeros(shape, jnp.int32)
    for prompt in range(prompts):
        span_of = jnp.where(column // length == prompt, spans_ref[base + prompt], span_of)
    later = (row // length == column // length) & (column > row) & (column % length < span_of)
    later = jnp.where(later, 1.0, 0.0).astype(bf16)
    remaining = sum(dot(later, part) for part in bf16_parts(rates, 3))
    row_wide = lax.broadcasted_iota(jnp.int32, decay_log.shape, 0)
    span_wide = jnp.zeros(decay_log.shape, jnp.int32)
    for prompt in range(prompts):
        span_wide = jnp.where(row_wide // length == prompt, spans_ref[base + prompt], span_wide)
    weighted = jnp.where(row_wide % length < span_wide, keys * jnp.exp(-remaining), 0.0).astype(bf16)
    columns = weighted.shape[1]
    out_ref[:, 0:length, :] = weighted.reshape(prompts, length, columns)
    out_ref[:, length:, :] = values.reshape(prompts, length, columns)


def factors(
    embeds,
    owners,
    lengths,
    length,
    opening_lagged_blend,
    lagged_blend_weights,
    blending_left_operand,
    blending_right_operands,
    fixed_fading_scores,
    fading_left_operand,
    fading_right_operand,
    address_projector,
    payload_projector,
):
    tokens, block_width = embeds[0].shape
    features = address_projector.shape[1]
    columns = address_projector.shape[0]
    blocks = len(embeds)
    rows = length * max(1, min(LANES // length, tokens // length))
    width = min(block_width, 512)
    rank = blending_right_operands.shape[1]
    whole = lambda *shape: pl.BlockSpec(shape, lambda i: (0,) * len(shape))
    return pl.pallas_call(
        functools.partial(factor_kernel, blocks=blocks, width=width, length=length, rank=rank),
        grid=(tokens // rows,),
        out_shape=jax.ShapeDtypeStruct((tokens // length, 2 * length, columns), bf16),
        in_specs=[SMEM, SMEM]
        + [pl.BlockSpec((rows, block_width), lambda i: (i, 0)) for _ in embeds]
        + [
            whole(1, features),
            whole(3, features),
            whole(3 * rank, features),
            whole(3, rank, features),
            whole(1, columns),
            whole(*fading_left_operand.shape),
            whole(*fading_right_operand.shape),
            whole(columns, features),
            whole(columns, features),
        ],
        out_specs=pl.BlockSpec((rows // length, 2 * length, columns), lambda i: (i, 0, 0)),
        scratch_shapes=[pltpu.VMEM((rows, features), f32)],
        cost_estimate=pl.CostEstimate(
            flops=4 * tokens * features * columns,
            bytes_accessed=4 * features * columns,
            transcendentals=0,
        ),
        name="factors",
    )(
        owners,
        lengths,
        *embeds,
        opening_lagged_blend.reshape(1, -1),
        lagged_blend_weights,
        blending_left_operand.T,
        blending_right_operands,
        fixed_fading_scores.reshape(1, -1),
        fading_left_operand,
        fading_right_operand,
        address_projector,
        payload_projector,
    )


def head_sums(x, ones, parts):
    wide = ones.shape[0]
    return jnp.concatenate(
        [
            sum(dot(part, ones) for part in bf16_parts(x[:, k : k + wide], parts))
            for k in range(0, x.shape[1], wide)
        ],
        axis=1,
    )


def decode_kernel(
    bank_ref,
    own_ref,
    other_ref,
    receptance_ref,
    key_ref,
    value_ref,
    fading_ref,
    gate_ref,
    reward_ref,
    gain_ref,
    bias_ref,
    out_ref,
    *,
    head,
    length,
):
    steps = receptance_ref.shape[1]
    wide = 2 * LANES
    row = lax.broadcasted_iota(jnp.int32, (wide, wide), 0)
    column = lax.broadcasted_iota(jnp.int32, (wide, wide), 1)
    ones = jnp.where(row // head == column // head, 1.0, 0.0).astype(bf16)
    reward = reward_ref[...]
    for bank, ref in ((bank_ref[0], own_ref), (bank_ref[1], other_ref)):
        parcels = [ref[k] for k in range(ref.shape[0])]
        both = parcels[0] if len(parcels) == 1 else jnp.concatenate(parcels, axis=1)
        keys = both[0:length].astype(f32)
        values = both[length:].astype(f32)
        receptance = receptance_ref[bank].astype(f32)
        new_keys = key_ref[bank].astype(f32)
        new_values = value_ref[bank].astype(f32)
        factor = jnp.exp(-jnp.exp(fading_ref[bank].astype(f32)))
        gate = gate_ref[bank].astype(f32)
        results = []
        decay = None
        held = []
        for step in range(steps):
            now = receptance[step : step + 1]
            query = now if decay is None else now * decay
            score = head_sums(keys * query, ones, 2)
            fresh = [now * item for item in held]
            fresh.append(now * reward * new_keys[step : step + 1])
            fresh += [jnp.zeros_like(now)] * (steps - len(fresh))
            near = head_sums(jnp.concatenate(fresh, axis=0), ones, 2)
            results.append(
                jnp.sum(score * values, axis=0, keepdims=True)
                + jnp.sum(near * new_values, axis=0, keepdims=True)
            )
            fade = factor[step : step + 1]
            decay = fade if decay is None else decay * fade
            held = [item * fade for item in held] + [new_keys[step : step + 1]]
        mixed = jnp.concatenate(results, axis=0)
        centred = mixed - head_sums(mixed, ones, 3) * (1.0 / head)
        spread = head_sums(centred * centred, ones, 3) * (1.0 / head)
        normed = centred * lax.rsqrt(spread + norm_eps)
        out = (normed * gain_ref[...] + bias_ref[...]) * (gate / (1.0 + jnp.exp(-gate)))
        out_ref[bank] = out.astype(bf16)


def decode(banks, own, other, streams, reward, gain, bias, head, length):
    shape = streams[0].shape
    return pl.pallas_call(
        functools.partial(decode_kernel, head=head, length=length),
        out_shape=jax.ShapeDtypeStruct(shape, bf16),
        in_specs=[SMEM] + [VMEM] * 10,
        out_specs=VMEM,
        name="decode",
    )(banks, own, other, *streams, reward, gain, bias)


def per_device(
    context_symbol_ids,
    context_symbol_spans,
    symbol_vector_lookup,
    opening_lagged_blend,
    lagged_blend_weights,
    blending_left_operand,
    blending_right_operands,
    fixed_fading_scores,
    fading_left_operand,
    fading_right_operand,
    address_projector,
    payload_projector,
    present_symbol_reward,
    cluster_scaling_weight,
    cluster_scaling_offset,
    generated_acceptance,
    generated_addresses,
    generated_payloads,
    generated_fading_scores,
    generated_valve_scores,
):
    wide = lax.axis_size("wide")
    narrow = lax.axis_size("narrow")
    place = lax.axis_index("wide")
    core = lax.axis_index("narrow")
    length = context_symbol_ids.shape[2]
    columns = symbol_vector_lookup.shape[0]
    head = present_symbol_reward.shape[1]
    lengths = context_symbol_spans.reshape(-1)

    picked = pick(symbol_vector_lookup, context_symbol_ids.reshape(-1))
    if wide <= 16 and columns % LANES == 0:
        embeds = [picked]
        for shift in range(1, wide):
            embeds.append(
                lax.ppermute(picked, "wide", [(i, (i + shift) % wide) for i in range(wide)])
            )
        owners = jnp.remainder(place - jnp.arange(wide, dtype=jnp.int32), wide)
    else:
        gathered = lax.all_gather(picked, "wide", axis=0)
        embeds = [gathered.transpose(1, 0, 2).reshape(picked.shape[0], wide * columns)]
        owners = jnp.zeros((1,), jnp.int32)
    parcel = factors(
        embeds,
        owners,
        lengths,
        length,
        opening_lagged_blend,
        lagged_blend_weights,
        blending_left_operand,
        blending_right_operands,
        fixed_fading_scores,
        fading_left_operand,
        fading_right_operand,
        address_projector,
        payload_projector,
    )
    handed = lax.all_to_all(parcel, "wide", split_axis=0, concat_axis=0, tiled=True)
    share = wide // narrow
    own = lax.dynamic_slice_in_dim(handed, core * share, share, 0)
    away = lax.dynamic_slice_in_dim(handed, (1 - core) * share, share, 0)
    other = lax.ppermute(away, "narrow", [(0, 1), (1, 0)])
    if columns % LANES:
        own, other = (
            x.transpose(1, 0, 2).reshape(1, 2 * length, share * columns) for x in (own, other)
        )
    streams = [
        x.reshape(x.shape[0], x.shape[2], x.shape[3])
        for x in (
            generated_acceptance,
            generated_addresses,
            generated_payloads,
            generated_fading_scores,
            generated_valve_scores,
        )
    ]
    part = share * columns
    take = lambda x: lax.dynamic_slice_in_dim(x.reshape(1, -1), core * part, part, 1)
    out = decode(
        jnp.stack([core, 1 - core]).astype(jnp.int32),
        own,
        other,
        streams,
        take(present_symbol_reward),
        take(cluster_scaling_weight),
        take(cluster_scaling_offset),
        head,
        length,
    )
    return out.reshape(generated_acceptance.shape)


def solution(mesh):
    placed = (
        P("narrow", "groups", None),
        P("narrow", "groups"),
        P("wide", None),
        P(),
        P(),
        P(),
        P(),
        P("wide"),
        P(),
        P(None, "wide"),
        P("wide", None),
        P("wide", None),
        P(),
        P(),
        P(),
        P(None, ("groups", "wide"), None, "narrow"),
        P(None, ("groups", "wide"), None, "narrow"),
        P(None, ("groups", "wide"), None, "narrow"),
        P(None, ("groups", "wide"), None, "narrow"),
        P(None, ("groups", "wide"), None, "narrow"),
    )
    return jax.shard_map(
        per_device,
        mesh=mesh,
        in_specs=placed,
        out_specs=P(None, ("groups", "wide"), None, "narrow"),
        check_vma=False,
    )
```

time: 182 us -> 82.4 us (0.45)
  local copies, waits for them, and re-layouts: 57.7 us -> 5.2 us
  waiting for transfers between devices: 66 us -> 14.5 us
  Pallas kernels: 0 us -> 34.6 us
  matrix products: 29.8 us -> 0 us
  starting transfers between devices: 3.77 us -> 26.6 us
  between operations: 13.8 us -> 0.08 us
  blocking collectives: 4.58 us -> 0 us
  other arithmetic: 4.89 us -> 1.13 us
    unnamed x33 -> x22, local copies, waits for them, and re-layouts: 44.4 us -> 1.42 us
    all_gather x1 -> x0, waiting for transfers between devices: 42.1 us -> none  [per_device(): gathered = lax.all_gather(picked, 'wide', axis=0, tiled=True).T]
    pallas_call x0 -> x3, Pallas kernels: none -> 34.6 us  [the longest x1 14.7 us: pick(): pl.pallas_call(functools.partial(pick_kernel, batch=batch), out_shape=jax...]
    dot_general x10 -> x0, matrix products: 29.8 us -> none  [the longest x4 13.7 us: generation_iterations(): jnp.einsum('...hi,...hij->...hj', present_acceptance, recurrent_memories,...]
    all_to_all x1, waiting for transfers between devices: 23.9 us -> 8.13 us  [per_device(): lax.all_to_all(parcel, 'wide', split_axis=0, concat_axis=0, tiled=True)]
    ppermute x0 -> x8, starting transfers between devices: none -> 14.7 us  [the longest x7 14.7 us: per_device(): lax.ppermute(picked, 'wide', [(i, (i + shift) % wide) for i in range(wide)])]
    all_to_all x1, starting transfers between devices: 3.77 us -> 12 us  [per_device(): lax.all_to_all(parcel, 'wide', split_axis=0, concat_axis=0, tiled=True)]
    ppermute x0 -> x8, waiting for transfers between devices: none -> 6.36 us  [the longest x7 6.36 us: per_device(): lax.ppermute(picked, 'wide', [(i, (i + shift) % wide) for i in range(wide)])]
  transfers between devices with their start and end apart: 2 -> 9, of which waited for: 2 -> 3; matrix products, arithmetic and copies ran while one was open for 0% -> 4% of each run, Pallas kernels for 0% -> 0%
where the time goes in v1:
time: 82.4 us; the launch traced here: 82.1 us
  Pallas kernels  34.6 us (42%)
  starting transfers between devices  26.6 us (32%)
  waiting for transfers between devices  14.5 us (18%)
  local copies, waits for them, and re-layouts  5.2 us (6%)
  other arithmetic  1.13 us (1%)
    pallas_call x1, Pallas kernels, pick(): pl.pallas_call(functools.partial(pick_kernel, batch=batch), out_shape=jax...  14.7 us
    ppermute x7, starting transfers between devices, per_device(): lax.ppermute(picked, 'wide', [(i, (i + shift) % wide) for i in range(wide)])  14.7 us
    pallas_call x1, Pallas kernels, factors(): pl.pallas_call(functools.partial(factor_kernel, blocks=blocks, width=widt...  12.1 us
    all_to_all x1, starting transfers between devices, per_device(): lax.all_to_all(parcel, 'wide', split_axis=0, concat_axis=0, tiled=True)  12 us
    all_to_all x1, waiting for transfers between devices, per_device(): lax.all_to_all(parcel, 'wide', split_axis=0, concat_axis=0, tiled=True)  8.13 us
    pallas_call x1, Pallas kernels, decode(): pl.pallas_call(functools.partial(decode_kernel, head=head, length=length)...  7.79 us
    ppermute x7, waiting for transfers between devices, per_device(): lax.ppermute(picked, 'wide', [(i, (i + shift) % wide) for i in range(wide)])  6.36 us
  transfers between devices with their start and end apart: 9, of which 3 were waited for; matrix products, arithmetic and copies ran while one was open for 4% of the time, Pallas kernels for 0%

profile of v1, /device:TPU:0, one launch (start us, length us, event | category | flops | bytes accessed | tf_op | source)
XLA Modules:
  0.0 82.1 jit_solution(16542490340164993995)
XLA Ops:
  0.0 1.3 %reshape.38.ids_ref = s32[128]{0:T(128)} reshape(s32[1,8,16]{2,1,0:T(8,128)} %param.20) | data formatting | bytes 1024 | tf_op jit(solution)/shard_map/reshape | solution.py:366
  1.3 14.7 %pick.1.refs_0_ = bf16[128,512]{1,0:T(8,128)(2,1)} custom-call(s32[128]{0:T(128)} %reshape.38.ids_ref, bf16[512,32768]{1,0:T(8,128)(2,1)} %table_ref.1), custom_call_target="tpu_custom_call" | custom-call | bytes 16777216 | tf_op jit(solution)/shard_map/pick/pallas_call | solution.py:89
  16.0 3.0 %collective-permute-start = (bf16[128,512]{1,0:T(8,128)(2,1)}, bf16[128,512]{1,0:T(8,128)(2,1)S(1)}, u32[]{:S(2)}, u32[]{:S(2)}) collective-permute-start(bf16[128,512]{1,0:T(8,128)(2,1)} %pick.1.refs_0_), channel_id=1, source_target_pairs={{0,2},{2,4},{4,6},{6,8},{8,10},{10,12},{12,14},{14,0},{1,3},{3,5},... | collective-permute-start | bytes 393224 | tf_op jit(solution)/shard_map/ppermute | solution.py:371
  19.0 1.6 %collective-permute-start.1 = (bf16[128,512]{1,0:T(8,128)(2,1)}, bf16[128,512]{1,0:T(8,128)(2,1)S(1)}, u32[]{:S(2)}, u32[]{:S(2)}) collective-permute-start(bf16[128,512]{1,0:T(8,128)(2,1)} %pick.1.refs_0_), channel_id=1, source_target_pairs={{0,4},{2,6},{4,8},{6,10},{8,12},{10,14},{12,0},{14,2},{1,5},{3,7},... | collective-permute-start | bytes 393224 | tf_op jit(solution)/shard_map/ppermute | solution.py:371
  20.6 2.5 %collective-permute-start.2 = (bf16[128,512]{1,0:T(8,128)(2,1)}, bf16[128,512]{1,0:T(8,128)(2,1)S(1)}, u32[]{:S(2)}, u32[]{:S(2)}) collective-permute-start(bf16[128,512]{1,0:T(8,128)(2,1)} %pick.1.refs_0_), channel_id=1, source_target_pairs={{0,6},{2,8},{4,10},{6,12},{8,14},{10,0},{12,2},{14,4},{1,7},{3,9},... | collective-permute-start | bytes 393224 | tf_op jit(solution)/shard_map/ppermute | solution.py:371
  23.2 1.2 %collective-permute-start.3 = (bf16[128,512]{1,0:T(8,128)(2,1)}, bf16[128,512]{1,0:T(8,128)(2,1)S(1)}, u32[]{:S(2)}, u32[]{:S(2)}) collective-permute-start(bf16[128,512]{1,0:T(8,128)(2,1)} %pick.1.refs_0_), channel_id=1, source_target_pairs={{0,8},{2,10},{4,12},{6,14},{8,0},{10,2},{12,4},{14,6},{1,9},{3,11}... | collective-permute-start | bytes 393224 | tf_op jit(solution)/shard_map/ppermute | solution.py:371
  24.4 2.6 %collective-permute-start.4 = (bf16[128,512]{1,0:T(8,128)(2,1)}, bf16[128,512]{1,0:T(8,128)(2,1)S(1)}, u32[]{:S(2)}, u32[]{:S(2)}) collective-permute-start(bf16[128,512]{1,0:T(8,128)(2,1)} %pick.1.refs_0_), channel_id=1, source_target_pairs={{0,10},{2,12},{4,14},{6,0},{8,2},{10,4},{12,6},{14,8},{1,11},{3,13... | collective-permute-start | bytes 393224 | tf_op jit(solution)/shard_map/ppermute | solution.py:371
  27.0 0.0 collective-permute-done.refs_1_
  27.0 0.0 copy-start
  27.0 1.6 %collective-permute-start.5 = (bf16[128,512]{1,0:T(8,128)(2,1)}, bf16[128,512]{1,0:T(8,128)(2,1)S(1)}, u32[]{:S(2)}, u32[]{:S(2)}) collective-permute-start(bf16[128,512]{1,0:T(8,128)(2,1)} %pick.1.refs_0_), channel_id=1, source_target_pairs={{0,12},{2,14},{4,0},{6,2},{8,4},{10,6},{12,8},{14,10},{1,13},{3,15... | collective-permute-start | bytes 393224 | tf_op jit(solution)/shard_map/ppermute | solution.py:371
  28.6 0.0 collective-permute-done.1.refs_2_
  28.6 2.1 %collective-permute-start.6 = (bf16[128,512]{1,0:T(8,128)(2,1)}, bf16[128,512]{1,0:T(8,128)(2,1)S(1)}, u32[]{:S(2)}, u32[]{:S(2)}) collective-permute-start(bf16[128,512]{1,0:T(8,128)(2,1)} %pick.1.refs_0_), channel_id=1, source_target_pairs={{0,14},{2,0},{4,2},{6,4},{8,6},{10,8},{12,10},{14,12},{1,15},{3,1}... | collective-permute-start | bytes 393224 | tf_op jit(solution)/shard_map/ppermute | solution.py:371
  30.7 0.5 and_select_fusion.owners_ref
  31.2 6.0 %collective-permute-done.2.refs_3_ = bf16[128,512]{1,0:T(8,128)(2,1)S(1)} collective-permute-done((bf16[128,512]{1,0:T(8,128)(2,1)}, bf16[128,512]{1,0:T(8,128)(2,1)S(1)}, u32[]{:S(2)}, u32[]{:S(2)}) %collective-permute-start.2) | collective-permute-done | bytes 131104 | tf_op jit(solution)/shard_map/ppermute | solution.py:371
  37.2 0.0 copy-start.2
  37.2 0.4 collective-permute-done.3.refs_4_
  37.5 0.0 copy-start.3
  37.5 0.0 collective-permute-done.4.refs_5_
  37.5 0.0 copy-start.4
  37.5 0.0 collective-permute-done.5.refs_6_
  37.5 0.0 copy-start.5
  37.6 0.0 collective-permute-done.6.refs_7_
  37.6 0.0 copy-start.6
  37.6 0.0 copy-done
  37.6 0.0 copy-done.1
  37.6 0.2 copy-done.2
  37.8 0.4 copy-done.3
  38.2 0.0 copy-done.4
  38.2 0.1 copy-done.5
  38.3 0.0 copy-done.6
  38.3 0.0 copy-start.8
  38.3 0.0 copy-start.10
  38.3 12.1 %factors.1 = bf16[8,32,512]{2,1,0:T(8,128)(2,1)} custom-call(s32[8]{0:T(128)} %and_select_fusion.owners_ref, s32[8]{0:T(128)} %bitcast.26, bf16[128,512]{1,0:T(8,128)(2,1)} %pick.1.refs_0_, bf16[128,512]{1,0:T(8,128)(2,1)} %copy-done, bf16[128,512]{1,0:T(8,128)(2,1)} %copy-done.1, bf16[128,512]{1,0:T(8,128)(2,1)} %copy-done.2, bf16[128,512]{1,0:T(8,128)(2,1)} %copy-done.3, ...), custom_call_target="tpu_custom_call" | custom-call | flops 1073741824 | bytes 8388608 | tf_op jit(solution)/shard_map/factors/pallas_call | solution.py:213
  50.5 12.0 %all-to-all-start = ((bf16[8,32,512]{2,1,0:T(8,128)(2,1)}), bf16[8,32,512]{2,1,0:T(8,128)(2,1)S(1)}, u32[]{:S(2)}, u32[]{:S(2)}) async-start(bf16[8,32,512]{2,1,0:T(8,128)(2,1)} %factors.1), calls=%async_computation | async-start | bytes 524288 | tf_op jit(solution)/shard_map/all_to_all | solution.py:393
  62.4 0.0 copy-done.8
  62.4 0.1 reshape.46
  62.5 8.1 %all-to-all-done = bf16[8,32,512]{2,1,0:T(8,128)(2,1)S(1)} async-done(((bf16[8,32,512]{2,1,0:T(8,128)(2,1)}), bf16[8,32,512]{2,1,0:T(8,128)(2,1)S(1)}, u32[]{:S(2)}, u32[]{:S(2)}) %all-to-all-start) | async-done | bytes 262176 | tf_op jit(solution)/shard_map/all_to_all | solution.py:393
  70.6 0.7 constant_dynamic-slice_fusion.1
  71.3 0.0 collective-permute-start.7
  71.3 0.6 constant_dynamic-slice_fusion.reward_ref
  71.9 0.0 copy-done.9
  71.9 0.6 dynamic-slice.6
  72.5 0.0 copy-done.10
  72.5 0.6 dynamic-slice.7
  73.1 0.6 pad_add_fusion.bank_ref
  73.7 0.0 collective-permute-done.7.other_ref
  73.7 0.6 copy-done.7
  74.3 7.8 %decode.1 = bf16[2,4,2048]{2,1,0:T(4,128)(2,1)} custom-call(s32[2]{0:T(128)} %pad_add_fusion.bank_ref, bf16[4,32,512]{2,1,0:T(8,128)(2,1)} %get-tuple-element.6.own_ref, bf16[4,32,512]{2,1,0:T(8,128)(2,1)} %copy-done.7, bf16[2,4,2048]{2,1,0:T(4,128)(2,1)} %bitcast.19, bf16[2,4,2048]{2,1,0:T(4,128)(2,1)} %bitcast.20, bf16[2,4,2048]{2,1,0:T(4,128)(2,1)} %bitcast.21, ...), custom_call_target="tpu_custom_call" | custom-call | tf_op jit(solution)/shard_map/decode/pallas_call | solution.py:326
  (3 shorter events, 0.0 us)
Async XLA Ops:
  16.0 11.0 %collective-permute-start = (bf16[128,512]{1,0:T(8,128)(2,1)}, bf16[128,512]{1,0:T(8,128)(2,1)S(1)}, u32[]{:S(2)}, u32[]{:S(2)}) collective-permute-start(bf16[128,512]{1,0:T(8,128)(2,1)} %pick.1.refs_0_), channel_id=1, source_target_pairs={{0,2},{2,4},{4,6},{6,8},{8,10},{10,12},{12,14},{14,0},{1,3},{3,5},... | collective-permute-start | bytes 393224 | tf_op jit(solution)/shard_map/ppermute | solution.py:371
  19.0 9.6 %collective-permute-start.1 = (bf16[128,512]{1,0:T(8,128)(2,1)}, bf16[128,512]{1,0:T(8,128)(2,1)S(1)}, u32[]{:S(2)}, u32[]{:S(2)}) collective-permute-start(bf16[128,512]{1,0:T(8,128)(2,1)} %pick.1.refs_0_), channel_id=1, source_target_pairs={{0,4},{2,6},{4,8},{6,10},{8,12},{10,14},{12,0},{14,2},{1,5},{3,7},... | collective-permute-start | bytes 393224 | tf_op jit(solution)/shard_map/ppermute | solution.py:371
  20.6 16.5 %collective-permute-start.2 = (bf16[128,512]{1,0:T(8,128)(2,1)}, bf16[128,512]{1,0:T(8,128)(2,1)S(1)}, u32[]{:S(2)}, u32[]{:S(2)}) collective-permute-start(bf16[128,512]{1,0:T(8,128)(2,1)} %pick.1.refs_0_), channel_id=1, source_target_pairs={{0,6},{2,8},{4,10},{6,12},{8,14},{10,0},{12,2},{14,4},{1,7},{3,9},... | collective-permute-start | bytes 393224 | tf_op jit(solution)/shard_map/ppermute | solution.py:371
  23.2 14.4 %collective-permute-start.3 = (bf16[128,512]{1,0:T(8,128)(2,1)}, bf16[128,512]{1,0:T(8,128)(2,1)S(1)}, u32[]{:S(2)}, u32[]{:S(2)}) collective-permute-start(bf16[128,512]{1,0:T(8,128)(2,1)} %pick.1.refs_0_), channel_id=1, source_target_pairs={{0,8},{2,10},{4,12},{6,14},{8,0},{10,2},{12,4},{14,6},{1,9},{3,11}... | collective-permute-start | bytes 393224 | tf_op jit(solution)/shard_map/ppermute | solution.py:371
  24.4 13.1 %collective-permute-start.4 = (bf16[128,512]{1,0:T(8,128)(2,1)}, bf16[128,512]{1,0:T(8,128)(2,1)S(1)}, u32[]{:S(2)}, u32[]{:S(2)}) collective-permute-start(bf16[128,512]{1,0:T(8,128)(2,1)} %pick.1.refs_0_), channel_id=1, source_target_pairs={{0,10},{2,12},{4,14},{6,0},{8,2},{10,4},{12,6},{14,8},{1,11},{3,13... | collective-permute-start | bytes 393224 | tf_op jit(solution)/shard_map/ppermute | solution.py:371
  27.0 10.5 %copy-start = (bf16[128,512]{1,0:T(8,128)(2,1)}, bf16[128,512]{1,0:T(8,128)(2,1)S(1)}, u32[]{:S(2)}) copy-start(bf16[128,512]{1,0:T(8,128)(2,1)S(1)} %collective-permute-done.refs_1_) | copy-start | bytes 393220
  27.0 10.5 %collective-permute-start.5 = (bf16[128,512]{1,0:T(8,128)(2,1)}, bf16[128,512]{1,0:T(8,128)(2,1)S(1)}, u32[]{:S(2)}, u32[]{:S(2)}) collective-permute-start(bf16[128,512]{1,0:T(8,128)(2,1)} %pick.1.refs_0_), channel_id=1, source_target_pairs={{0,12},{2,14},{4,0},{6,2},{8,4},{10,6},{12,8},{14,10},{1,13},{3,15... | collective-permute-start | bytes 393224 | tf_op jit(solution)/shard_map/ppermute | solution.py:371
  28.6 9.0 %copy-start.1 = (bf16[128,512]{1,0:T(8,128)(2,1)}, bf16[128,512]{1,0:T(8,128)(2,1)S(1)}, u32[]{:S(2)}) copy-start(bf16[128,512]{1,0:T(8,128)(2,1)S(1)} %collective-permute-done.1.refs_2_) | copy-start | bytes 393220
  28.6 8.9 %collective-permute-start.6 = (bf16[128,512]{1,0:T(8,128)(2,1)}, bf16[128,512]{1,0:T(8,128)(2,1)S(1)}, u32[]{:S(2)}, u32[]{:S(2)}) collective-permute-start(bf16[128,512]{1,0:T(8,128)(2,1)} %pick.1.refs_0_), channel_id=1, source_target_pairs={{0,14},{2,0},{4,2},{6,4},{8,6},{10,8},{12,10},{14,12},{1,15},{3,1}... | collective-permute-start | bytes 393224 | tf_op jit(solution)/shard_map/ppermute | solution.py:371
  37.2 0.7 copy-start.2
  37.5 0.6 copy-start.3
  37.5 0.7 copy-start.4
  37.5 0.8 copy-start.5
  37.6 0.8 copy-start.6
  38.3 24.1 %copy-start.8 = (f32[64,64]{1,0:T(8,128)S(1)}, f32[64,64]{1,0:T(8,128)}, u32[]{:S(2)}) copy-start(f32[64,64]{1,0:T(8,128)} %param.32) | copy-start | bytes 49156
  38.3 33.6 %copy-start.9 = (f32[4096]{0:T(1024)S(1)}, f32[4096]{0:T(1024)}, u32[]{:S(2)}) copy-start(f32[4096]{0:T(1024)} %param.33) | copy-start | bytes 49156
  38.3 34.2 %copy-start.10 = (f32[4096]{0:T(1024)S(1)}, f32[4096]{0:T(1024)}, u32[]{:S(2)}) copy-start(f32[4096]{0:T(1024)} %param.34) | copy-start | bytes 49156
  50.5 20.2 %all-to-all-start = ((bf16[8,32,512]{2,1,0:T(8,128)(2,1)}), bf16[8,32,512]{2,1,0:T(8,128)(2,1)S(1)}, u32[]{:S(2)}, u32[]{:S(2)}) async-start(bf16[8,32,512]{2,1,0:T(8,128)(2,1)} %factors.1), calls=%async_computation | async-start | bytes 524288 | tf_op jit(solution)/shard_map/all_to_all | solution.py:393
  71.3 2.4 %collective-permute-start.7 = (bf16[4,32,512]{2,1,0:T(8,128)(2,1)S(1)}, bf16[4,32,512]{2,1,0:T(8,128)(2,1)S(1)}, u32[]{:S(2)}, u32[]{:S(2)}) collective-permute-start(bf16[4,32,512]{2,1,0:T(8,128)(2,1)S(1)} %get-tuple-element.5), channel_id=1, source_target_pairs={{0,1},{1,0},{2,3},{3,2},{4,5},{5,4},{6,7},{7,6},{8,9},{9,8},{10,11... | collective-permute-start | bytes 393224 | tf_op jit(solution)/shard_map/ppermute | solution.py:397
  73.7 0.7 copy-start.7

commit v2 on v1

v2 whole, which is shorter than its diff:
```python
import functools

import jax
import jax.numpy as jnp
from jax import lax
from jax.experimental import pallas as pl
from jax.experimental.pallas import tpu as pltpu
from jax.sharding import PartitionSpec as P

norm_eps = 0.00064
LANES = 128
bf16 = jnp.bfloat16
f32 = jnp.float32
NT = (((1,), (1,)), ((), ()))
VMEM = pl.BlockSpec(memory_space=pltpu.VMEM)
SMEM = pl.BlockSpec(memory_space=pltpu.SMEM)
ANY = pl.BlockSpec(memory_space=pl.ANY)


def dot(a, b):
    return jnp.dot(a, b, preferred_element_type=f32)


def dot_nt(a, b):
    return lax.dot_general(a, b, NT, preferred_element_type=f32)


def bf16_parts(x, count):
    parts = []
    for _ in range(count - 1):
        head = x.astype(bf16)
        parts.append(head)
        x = x - head.astype(f32)
    parts.append(x.astype(bf16))
    return parts


def pick_kernel(ids_ref, table_ref, out_ref, held, placed, sems, *, batch, ahead):
    tokens, features, lanes = held.shape
    length = ids_ref.shape[1]
    batches = tokens // batch
    rows = min(features, 128)
    lane = lax.broadcasted_iota(jnp.int32, (rows, lanes), 1)

    def start(group):
        def one(step, carry):
            token = group * batch + step
            block = ids_ref[token // length, token % length] // lanes
            pltpu.make_async_copy(
                table_ref.at[:, pl.ds(pl.multiple_of(block * lanes, lanes), lanes)],
                held.at[token],
                sems.at[group],
            ).start()
            return carry

        lax.fori_loop(0, batch, one, 0)

    for group in range(min(ahead, batches)):
        start(group)
    for group in range(batches):
        first = group * batch
        slot = first // lanes
        here = held.at[pl.ds(first, batch)]
        pltpu.make_async_copy(here, here, sems.at[group]).wait()
        if group + ahead < batches:
            start(group + ahead)
        for strip in range(0, features, rows):
            total = placed[slot, strip : strip + rows, :]
            for step in range(batch):
                token = first + step
                target = token % lanes
                column = ids_ref[token // length, token % length] % lanes
                moved = pltpu.roll(
                    held[token, strip : strip + rows, :], jnp.remainder(target - column, lanes), 1
                )
                total = jnp.where(lane == target, moved, total)
            placed[slot, strip : strip + rows, :] = total
    for slot in range(placed.shape[0]):
        out_ref[slot * lanes : (slot + 1) * lanes, :] = placed[slot].T


def pick(table, ids):
    features = table.shape[0]
    tokens = ids.shape[0] * ids.shape[1]
    batch = 16
    size = tokens * features * LANES * 2
    return pl.pallas_call(
        functools.partial(pick_kernel, batch=batch, ahead=4),
        out_shape=jax.ShapeDtypeStruct((tokens, features), bf16),
        in_specs=[SMEM, ANY],
        out_specs=VMEM,
        scratch_shapes=[
            pltpu.VMEM((tokens, features, LANES), bf16),
            pltpu.VMEM((tokens // LANES, features, LANES), bf16),
            pltpu.SemaphoreType.DMA((tokens // batch,)),
        ],
        cost_estimate=pl.CostEstimate(flops=0, bytes_accessed=size, transcendentals=0),
        compiler_params=pltpu.CompilerParams(vmem_limit_bytes=size + (6 << 20)),
        name="pick",
    )(ids, table)


def factor_kernel(earlier_ref, spans_ref, *refs, offsets, single, width, length, rank):
    blocks = len(offsets)
    place = lax.axis_index("wide") if blocks > 1 else 0
    embeds = refs[:blocks]
    (
        opening_ref,
        lagged_ref,
        left_ref,
        right_ref,
        fixed_ref,
        decay_left_ref,
        decay_right_ref,
        key_ref,
        value_ref,
        out_ref,
        gap_ref,
    ) = refs[blocks:]
    rows = embeds[0].shape[0]
    places = lax.broadcasted_iota(jnp.int32, (rows, width), 0) % length
    first = places == 0
    strips = embeds[0].shape[1] // width

    def spots():
        for block in range(blocks):
            base = (place ^ offsets[block]) * embeds[block].shape[1] if blocks > 1 else 0
            for strip in range(strips):
                column = base + strip * width
                where = pl.ds(pl.multiple_of(column, width) if blocks > 1 else column, width)
                yield block * strips + strip, embeds[block], slice(strip * width, (strip + 1) * width), where

    hidden = None
    for index, ref, here, there in spots():
        current = ref[:, here].astype(f32)
        gap = jnp.where(first, 0.0, pltpu.roll(current, 1, 0)) - current
        gap_ref[:, index * width : (index + 1) * width] = gap
        mixed = (current + gap * opening_ref[:, there]).astype(bf16)
        part = dot_nt(mixed, left_ref[:, there])
        hidden = part if hidden is None else hidden + part
    hidden = jnp.tanh(hidden).astype(bf16)
    lows = [hidden[:, j * rank : (j + 1) * rank] for j in range(3)]
    sums = [None, None, None]
    for index, ref, here, there in spots():
        current = ref[:, here].astype(f32)
        gap = gap_ref[:, index * width : (index + 1) * width]
        for j in range(3):
            shift = lagged_ref[j : j + 1, there] + dot(lows[j], right_ref[j, :, there])
            branch = (current + gap * shift).astype(bf16)
            if j == 0:
                part = dot(branch, decay_left_ref[there, :])
            else:
                part = dot_nt(branch, (key_ref, value_ref)[j - 1][:, there])
            sums[j] = part if sums[j] is None else sums[j] + part
    decay_hidden = jnp.tanh(sums[0]).astype(bf16)
    decay_log = fixed_ref[...] + dot(decay_hidden, decay_right_ref[...])
    keys = sums[1].astype(bf16).astype(f32)
    values = sums[2].astype(bf16)
    rates = jnp.exp(decay_log)
    shape = (rows, rows)
    row = lax.broadcasted_iota(jnp.int32, shape, 0)
    column = lax.broadcasted_iota(jnp.int32, shape, 1)
    prompts = rows // length
    base = 0 if single else pl.program_id(0) * prompts
    span_of = jnp.zeros(shape, jnp.int32)
    for prompt in range(prompts):
        span_of = jnp.where(column // length == prompt, spans_ref[base + prompt], span_of)
    later = (row // length == column // length) & (column > row) & (column % length < span_of)
    later = jnp.where(later, 1.0, 0.0).astype(bf16)
    remaining = sum(dot(later, part) for part in bf16_parts(rates, 3))
    row_wide = lax.broadcasted_iota(jnp.int32, decay_log.shape, 0)
    span_wide = jnp.zeros(decay_log.shape, jnp.int32)
    for prompt in range(prompts):
        span_wide = jnp.where(row_wide // length == prompt, spans_ref[base + prompt], span_wide)
    weighted = jnp.where(row_wide % length < span_wide, keys * jnp.exp(-remaining), 0.0).astype(bf16)
    columns = weighted.shape[1]
    out_ref[:, 0:length, :] = weighted.reshape(prompts, length, columns)
    out_ref[:, length:, :] = values.reshape(prompts, length, columns)


def factors(
    earlier,
    embeds,
    offsets,
    lengths,
    length,
    opening_lagged_blend,
    lagged_blend_weights,
    blending_left_operand,
    blending_right_operands,
    fixed_fading_scores,
    fading_left_operand,
    fading_right_operand,
    address_projector,
    payload_projector,
):
    tokens, block_width = embeds[0].shape
    features = address_projector.shape[1]
    columns = address_projector.shape[0]
    rows = length * max(1, min(LANES // length, tokens // length))
    single = rows == tokens
    width = min(block_width, 512)
    rank = blending_right_operands.shape[1]
    weights = (
        opening_lagged_blend.reshape(1, -1),
        lagged_blend_weights,
        blending_left_operand.T,
        blending_right_operands,
        fixed_fading_scores.reshape(1, -1),
        fading_left_operand,
        fading_right_operand,
        address_projector,
        payload_projector,
    )
    out = jax.ShapeDtypeStruct((tokens // length, 2 * length, columns), bf16)
    if single:
        places = dict(in_specs=[ANY, SMEM] + [VMEM] * (len(embeds) + len(weights)), out_specs=VMEM)
        limit = 20 << 20
    else:
        kept = [pl.BlockSpec(x.shape, lambda i, rank=x.ndim: (0,) * rank) for x in weights]
        places = dict(
            grid=(tokens // rows,),
            in_specs=[ANY, SMEM]
            + [pl.BlockSpec((rows, block_width), lambda i: (i, 0)) for _ in embeds]
            + kept,
            out_specs=pl.BlockSpec((rows // length,) + out.shape[1:], lambda i: (i, 0, 0)),
        )
        limit = 48 << 20
    return pl.pallas_call(
        functools.partial(
            factor_kernel, offsets=offsets, single=single, width=width, length=length, rank=rank
        ),
        out_shape=out,
        scratch_shapes=[pltpu.VMEM((rows, features), f32)],
        cost_estimate=pl.CostEstimate(
            flops=4 * tokens * features * columns,
            bytes_accessed=4 * features * columns,
            transcendentals=0,
        ),
        compiler_params=pltpu.CompilerParams(vmem_limit_bytes=limit),
        name="factors",
        **places,
    )(earlier, lengths, *embeds, *weights)


def head_ones(wide, head):
    row = lax.broadcasted_iota(jnp.int32, (wide, wide), 0)
    column = lax.broadcasted_iota(jnp.int32, (wide, wide), 1)
    return jnp.where(row // head == column // head, 1.0, 0.0).astype(bf16)


def head_sums(x, ones, parts):
    wide = ones.shape[0]
    count = x.shape[0]
    tall = jnp.concatenate([x[:, k : k + wide] for k in range(0, x.shape[1], wide)], axis=0)
    total = sum(dot(part, ones) for part in bf16_parts(tall, parts))
    return jnp.concatenate(
        [total[k : k + count] for k in range(0, total.shape[0], count)], axis=1
    )


def local_kernel(
    receptance_ref,
    key_ref,
    value_ref,
    fading_ref,
    gate_ref,
    reward_ref,
    query_ref,
    near_ref,
    open_ref,
    *,
    head,
):
    banks, steps, width = receptance_ref.shape
    core = lax.axis_index("narrow")

    def flat(ref):
        return jnp.concatenate([ref[bank].astype(f32) for bank in range(banks)], axis=0)

    receptance, keys, values, gate = (
        flat(ref) for ref in (receptance_ref, key_ref, value_ref, gate_ref)
    )
    factor = jnp.exp(-jnp.exp(flat(fading_ref)))
    step = lax.broadcasted_iota(jnp.int32, receptance.shape, 0) % steps
    ones = head_ones(2 * LANES, head)
    reward = reward_ref[:, pl.ds(pl.multiple_of(core * width, LANES), width)]

    def earlier(x, count, fill):
        return jnp.where(step >= count, pltpu.roll(x, count, 0), fill)

    near = head_sums(receptance * reward * keys, ones, 3) * values
    query = receptance
    for count in range(1, steps):
        pair = query * earlier(keys, count, 0.0)
        near = near + head_sums(pair, ones, 3) * earlier(values, count, 0.0)
        query = query * earlier(factor, count, 1.0)
    query_ref[...] = query
    near_ref[...] = near
    open_ref[...] = gate / (1.0 + jnp.exp(-gate))


def local(streams, reward, head):
    banks, steps, width = streams[0].shape
    shape = jax.ShapeDtypeStruct((banks * steps, width), f32)
    return pl.pallas_call(
        functools.partial(local_kernel, head=head),
        out_shape=(shape,) * 3,
        in_specs=[VMEM] * 6,
        out_specs=(VMEM,) * 3,
        cost_estimate=pl.CostEstimate(
            flops=banks * steps * steps * width * 1000,
            bytes_accessed=banks * steps * width * 22,
            transcendentals=0,
        ),
        compiler_params=pltpu.CompilerParams(vmem_limit_bytes=8 << 20),
        name="local",
    )(*streams, reward)


def decode_kernel(
    handed_ref,
    other_ref,
    query_ref,
    near_ref,
    open_ref,
    gain_ref,
    bias_ref,
    out_ref,
    kept,
    tall,
    *,
    head,
    length,
):
    banks, steps, width = out_ref.shape
    share, _, columns = other_ref.shape
    core = lax.axis_index("narrow")
    for k in range(share):
        lanes = slice(k * columns, (k + 1) * columns)
        kept[core, :, lanes] = handed_ref[core * share + k].astype(f32)
        kept[1 - core, :, lanes] = other_ref[k].astype(f32)
    wide = 2 * LANES
    chunks = width // wide
    rows = banks * steps
    ones = head_ones(wide, head)
    query = query_ref[...]
    first = lax.broadcasted_iota(jnp.int32, query.shape, 0) < steps

    def line(place):
        return jnp.where(first, kept[0, place : place + 1, :], kept[1, place : place + 1, :])

    for place in range(0, length, 2):
        pair = jnp.concatenate([query * line(place), query * line(place + 1)], axis=0)
        for part, x in enumerate(bf16_parts(pair, 2)):
            for k in range(chunks):
                base = k * length * rows + place * rows
                tall[base : base + 2 * rows, part * wide : (part + 1) * wide] = x[
                    :, k * wide : (k + 1) * wide
                ]
    scores = dot(tall[...], jnp.concatenate([ones, ones], axis=0))
    mixed = near_ref[...]
    for place in range(length):
        base = [k * length * rows + place * rows for k in range(chunks)]
        score = jnp.concatenate([scores[b : b + rows] for b in base], axis=1)
        mixed = mixed + score * line(length + place)
    centred = mixed - head_sums(mixed, ones, 3) * (1.0 / head)
    spread = head_sums(centred * centred, ones, 3) * (1.0 / head)
    normed = centred * lax.rsqrt(spread + norm_eps)
    here = pl.ds(pl.multiple_of(core * width, LANES), width)
    out = ((normed * gain_ref[:, here] + bias_ref[:, here]) * open_ref[...]).astype(bf16)
    for bank in range(banks):
        out_ref[bank] = out[bank * steps : (bank + 1) * steps]


def decode(handed, other, prepared, gain, bias, shape, head, length):
    rows = shape[0] * shape[1]
    chunks = shape[2] // (2 * LANES)
    return pl.pallas_call(
        functools.partial(decode_kernel, head=head, length=length),
        out_shape=jax.ShapeDtypeStruct(shape, bf16),
        in_specs=[VMEM] * 7,
        out_specs=VMEM,
        scratch_shapes=[
            pltpu.VMEM((shape[0], 2 * length, shape[2]), f32),
            pltpu.VMEM((chunks * length * rows, 4 * LANES), bf16),
        ],
        compiler_params=pltpu.CompilerParams(vmem_limit_bytes=12 << 20),
        name="decode",
    )(handed, other, *prepared, gain, bias)


def gather_plan(wide):
    top = wide // 2
    plan = []
    for offset in sorted(range(1, wide), key=lambda o: (top < o < wide - 1, -(o == top), -(o == wide - 1))):
        if top < offset < wide - 1:
            plan.append((offset, top, offset ^ top))
        else:
            plan.append((offset, 0, offset))
    return plan


def per_device(
    context_symbol_ids,
    context_symbol_spans,
    symbol_vector_lookup,
    opening_lagged_blend,
    lagged_blend_weights,
    blending_left_operand,
    blending_right_operands,
    fixed_fading_scores,
    fading_left_operand,
    fading_right_operand,
    address_projector,
    payload_projector,
    present_symbol_reward,
    cluster_scaling_weight,
    cluster_scaling_offset,
    generated_acceptance,
    generated_addresses,
    generated_payloads,
    generated_fading_scores,
    generated_valve_scores,
):
    wide = lax.axis_size("wide")
    narrow = lax.axis_size("narrow")
    core = lax.axis_index("narrow")
    length = context_symbol_ids.shape[2]
    columns = symbol_vector_lookup.shape[0]
    head = present_symbol_reward.shape[1]
    lengths = context_symbol_spans.reshape(-1)

    streams = [
        x.reshape(x.shape[0], x.shape[2], x.shape[3])
        for x in (
            generated_acceptance,
            generated_addresses,
            generated_payloads,
            generated_fading_scores,
            generated_valve_scores,
        )
    ]
    picked = pick(symbol_vector_lookup, context_symbol_ids[0])
    weights = (
        opening_lagged_blend,
        lagged_blend_weights,
        blending_left_operand,
        blending_right_operands,
        fixed_fading_scores,
        fading_left_operand,
        fading_right_operand,
        address_projector,
        payload_projector,
    )
    if wide <= 16 and wide & (wide - 1) == 0 and columns % LANES == 0:
        held = {0: picked}
        for offset, source, hop in gather_plan(wide):
            held[offset] = lax.ppermute(
                held[source], "wide", [(i, i ^ hop) for i in range(wide)]
            )
        offsets = tuple(sorted(held))
        embeds = [held[offset] for offset in offsets]
    else:
        gathered = lax.all_gather(picked, "wide", axis=0)
        embeds = [gathered.transpose(1, 0, 2).reshape(picked.shape[0], wide * columns)]
        offsets = (0,)
    prepared = local(streams, present_symbol_reward.reshape(1, -1), head)
    parcel = factors(prepared[0], embeds, offsets, lengths, length, *weights)
    handed = lax.all_to_all(parcel, "wide", split_axis=0, concat_axis=0, tiled=True)
    share = wide // narrow
    away = lax.dynamic_slice_in_dim(handed, (1 - core) * share, share, 0)
    other = lax.ppermute(away, "narrow", [(0, 1), (1, 0)])
    if columns % LANES:
        handed = handed.reshape(narrow, share, 2 * length, columns).transpose(0, 2, 1, 3)
        handed = handed.reshape(narrow, 2 * length, share * columns)
        other = other.transpose(1, 0, 2).reshape(1, 2 * length, share * columns)
    out = decode(
        handed,
        other,
        prepared,
        cluster_scaling_weight.reshape(1, -1),
        cluster_scaling_offset.reshape(1, -1),
        streams[0].shape,
        head,
        length,
    )
    return out.reshape(generated_acceptance.shape)


def solution(mesh):
    placed = (
        P("narrow", "groups", None),
        P("narrow", "groups"),
        P("wide", None),
        P(),
        P(),
        P(),
        P(),
        P("wide"),
        P(),
        P(None, "wide"),
        P("wide", None),
        P("wide", None),
        P(),
        P(),
        P(),
        P(None, ("groups", "wide"), None, "narrow"),
        P(None, ("groups", "wide"), None, "narrow"),
        P(None, ("groups", "wide"), None, "narrow"),
        P(None, ("groups", "wide"), None, "narrow"),
        P(None, ("groups", "wide"), None, "narrow"),
    )
    return jax.shard_map(
        per_device,
        mesh=mesh,
        in_specs=placed,
        out_specs=P(None, ("groups", "wide"), None, "narrow"),
        check_vma=False,
    )
```

time: 82.4 us -> 66.9 us (0.81)
  Pallas kernels: 34.6 us -> 18.9 us
  local copies, waits for them, and re-layouts: 5.2 us -> 17.4 us
  starting transfers between devices: 26.6 us -> 16.8 us
  waiting for transfers between devices: 14.5 us -> 12.7 us
  other arithmetic: 1.13 us -> 0 us
    unnamed x22 -> x50, local copies, waits for them, and re-layouts: 1.42 us -> 17.3 us
    pallas_call x2 -> x3, Pallas kernels: 26.8 us -> 17.2 us  [the longest x1 8.66 us: pick(): pl.pallas_call(functools.partial(pick_kernel, batch=batch, ahead=4), out_...]
    all_to_all x1, starting transfers between devices: 12 us -> 4.63 us  [per_device(): lax.all_to_all(parcel, 'wide', split_axis=0, concat_axis=0, tiled=True)]
    pallas_call x1, Pallas kernels: 7.79 us -> 1.65 us  [decode(): pl.pallas_call(functools.partial(decode_kernel, head=head, length=length)...]
    ppermute x7, waiting for transfers between devices: 6.36 us -> 2.27 us  [per_device(): lax.ppermute(held[source], 'wide', [(i, i ^ hop) for i in range(wide)])]
    ppermute x7, starting transfers between devices: 14.7 us -> 12.1 us  [per_device(): lax.ppermute(held[source], 'wide', [(i, i ^ hop) for i in range(wide)])]
    ppermute x1, waiting for transfers between devices: 0.01 us -> 1.33 us  [per_device(): other = lax.ppermute(away, 'narrow', [(0, 1), (1, 0)])]
    reshape x2 -> x1, local copies, waits for them, and re-layouts: 1.36 us -> 0.09 us  [per_device(): prepared = local(streams, present_symbol_reward.reshape(1, -1), head)]
  transfers between devices with their start and end apart: 9 -> 9, of which waited for: 3 -> 6; matrix products, arithmetic and copies ran while one was open for 4% -> 0% of each run, Pallas kernels for 0% -> 1%
where the time goes in v2:
time: 66.9 us; the launch traced here: 65.9 us
  Pallas kernels  18.9 us (28%)
  local copies, waits for them, and re-layouts  17.4 us (26%)
  starting transfers between devices  16.8 us (25%)
  waiting for transfers between devices  12.7 us (19%)
    unnamed x50, local copies, waits for them, and re-layouts  17.3 us
    ppermute x7, starting transfers between devices, per_device(): lax.ppermute(held[source], 'wide', [(i, i ^ hop) for i in range(wide)])  12.1 us
    all_to_all x1, waiting for transfers between devices, per_device(): lax.all_to_all(parcel, 'wide', split_axis=0, concat_axis=0, tiled=True)  9.1 us
    pallas_call x1, Pallas kernels, pick(): pl.pallas_call(functools.partial(pick_kernel, batch=batch, ahead=4), out_...  8.66 us
    pallas_call x1, Pallas kernels, factors(): pl.pallas_call(functools.partial(factor_kernel, offsets=offsets, single=s...  8.16 us
    all_to_all x1, starting transfers between devices, per_device(): lax.all_to_all(parcel, 'wide', split_axis=0, concat_axis=0, tiled=True)  4.63 us
    ppermute x7, waiting for transfers between devices, per_device(): lax.ppermute(held[source], 'wide', [(i, i ^ hop) for i in range(wide)])  2.27 us
    pallas_call x1, Pallas kernels, decode(): pl.pallas_call(functools.partial(decode_kernel, head=head, length=length)...  1.65 us
  transfers between devices with their start and end apart: 9, of which 6 were waited for; matrix products, arithmetic and copies ran while one was open for 0% of the time, Pallas kernels for 1%

profile of v2, /device:TPU:0, one launch (start us, length us, event | category | flops | bytes accessed | tf_op | source)
XLA Modules:
  0.0 65.9 jit_solution(1082079857174898808)
XLA Ops:
  0.0 0.7 %copy-done.16 = s32[1,8,16]{2,1,0:T(8,128)S(1)} copy-done((s32[1,8,16]{2,1,0:T(8,128)S(1)}, s32[1,8,16]{2,1,0:T(8,128)}, u32[]{:S(2)}) %copy-start.16) | copy-done | bytes 536
  0.7 0.0 copy-start.8
  0.7 8.7 %pick.1.refs_0_ = bf16[128,512]{1,0:T(8,128)(2,1)S(1)} custom-call(s32[8,16]{1,0:T(8,128)S(1)} %bitcast.19, bf16[512,32768]{1,0:T(8,128)(2,1)} %table_ref.1), custom_call_target="tpu_custom_call" | custom-call | bytes 16777216 | tf_op jit(solution)/shard_map/pick/pallas_call | solution.py:87
  9.4 4.1 %collective-permute-start.3 = (bf16[128,512]{1,0:T(8,128)(2,1)S(1)}, bf16[128,512]{1,0:T(8,128)(2,1)}, u32[]{:S(2)}, u32[]{:S(2)}) collective-permute-start(bf16[128,512]{1,0:T(8,128)(2,1)S(1)} %pick.1.refs_0_), channel_id=1, source_target_pairs={{0,8},{2,10},{4,12},{6,14},{8,0},{10,2},{12,4},{14,6},{1,9},{3,11}... | collective-permute-start | bytes 393224 | tf_op jit(solution)/shard_map/ppermute | solution.py:459
  13.5 1.5 %collective-permute-start = (bf16[128,512]{1,0:T(8,128)(2,1)S(1)}, bf16[128,512]{1,0:T(8,128)(2,1)S(1)}, u32[]{:S(2)}, u32[]{:S(2)}) collective-permute-start(bf16[128,512]{1,0:T(8,128)(2,1)S(1)} %pick.1.refs_0_), channel_id=1, source_target_pairs={{0,2},{2,0},{4,6},{6,4},{8,10},{10,8},{12,14},{14,12},{1,3},{3,1},... | collective-permute-start | bytes 393224 | tf_op jit(solution)/shard_map/ppermute | solution.py:459
  15.0 1.6 %collective-permute-start.1 = (bf16[128,512]{1,0:T(8,128)(2,1)S(1)}, bf16[128,512]{1,0:T(8,128)(2,1)}, u32[]{:S(2)}, u32[]{:S(2)}) collective-permute-start(bf16[128,512]{1,0:T(8,128)(2,1)S(1)} %pick.1.refs_0_), channel_id=1, source_target_pairs={{0,4},{2,6},{4,0},{6,2},{8,12},{10,14},{12,8},{14,10},{1,5},{3,7},... | collective-permute-start | bytes 393224 | tf_op jit(solution)/shard_map/ppermute | solution.py:459
  16.6 0.4 collective-permute-start.2
  17.0 2.3 %collective-permute-start.6 = (bf16[128,512]{1,0:T(8,128)(2,1)S(1)}, bf16[128,512]{1,0:T(8,128)(2,1)}, u32[]{:S(2)}, u32[]{:S(2)}) collective-permute-start(bf16[128,512]{1,0:T(8,128)(2,1)S(1)} %pick.1.refs_0_), channel_id=1, source_target_pairs={{0,14},{2,12},{4,10},{6,8},{8,6},{10,4},{12,2},{14,0},{1,15},{3,13... | collective-permute-start | bytes 393224 | tf_op jit(solution)/shard_map/ppermute | solution.py:459
  19.3 0.7 %collective-permute-done.3.refs_4_ = bf16[128,512]{1,0:T(8,128)(2,1)} collective-permute-done((bf16[128,512]{1,0:T(8,128)(2,1)S(1)}, bf16[128,512]{1,0:T(8,128)(2,1)}, u32[]{:S(2)}, u32[]{:S(2)}) %collective-permute-start.3) | collective-permute-done | bytes 131104 | tf_op jit(solution)/shard_map/ppermute | solution.py:459
  20.0 2.1 %collective-permute-start.4 = (bf16[128,512]{1,0:T(8,128)(2,1)}, bf16[128,512]{1,0:T(8,128)(2,1)}, u32[]{:S(2)}, u32[]{:S(2)}) collective-permute-start(bf16[128,512]{1,0:T(8,128)(2,1)} %collective-permute-done.3.refs_4_), channel_id=1, source_target_pairs={{0,2},{2,0},{4,6},{6,4},{8,10},{10,8},{12,14},{14,12},{1,3},{3,1},... | collective-permute-start | bytes 393224 | tf_op jit(solution)/shard_map/ppermute | solution.py:459
  22.1 0.0 collective-permute-done.refs_1_
  22.1 0.6 copy-done.6
  22.7 0.1 collective-permute-start.5
  22.8 0.0 copy-done.24
  22.8 0.1 reshape.41.reward_ref
  22.9 0.0 copy-start.19
  22.9 0.7 %copy-done.19 = bf16[2,1,4,2048]{3,2,1,0:T(4,128)(2,1)S(1)} copy-done((bf16[2,1,4,2048]{3,2,1,0:T(4,128)(2,1)S(1)}, bf16[2,1,4,2048]{3,2,1,0:T(4,128)(2,1)}, u32[]{:S(2)}) %copy-start.19) | copy-done | bytes 32792
  23.7 0.8 %copy-done.20 = bf16[2,1,4,2048]{3,2,1,0:T(4,128)(2,1)S(1)} copy-done((bf16[2,1,4,2048]{3,2,1,0:T(4,128)(2,1)S(1)}, bf16[2,1,4,2048]{3,2,1,0:T(4,128)(2,1)}, u32[]{:S(2)}) %copy-start.20) | copy-done | bytes 32792
  24.4 0.8 %copy-done.21 = bf16[2,1,4,2048]{3,2,1,0:T(4,128)(2,1)S(1)} copy-done((bf16[2,1,4,2048]{3,2,1,0:T(4,128)(2,1)S(1)}, bf16[2,1,4,2048]{3,2,1,0:T(4,128)(2,1)}, u32[]{:S(2)}) %copy-start.21) | copy-done | bytes 32792
  25.2 0.8 %copy-done.22 = bf16[2,1,4,2048]{3,2,1,0:T(4,128)(2,1)S(1)} copy-done((bf16[2,1,4,2048]{3,2,1,0:T(4,128)(2,1)S(1)}, bf16[2,1,4,2048]{3,2,1,0:T(4,128)(2,1)}, u32[]{:S(2)}) %copy-start.22) | copy-done | bytes 32792
  26.0 0.8 %copy-done.23 = bf16[2,1,4,2048]{3,2,1,0:T(4,128)(2,1)S(1)} copy-done((bf16[2,1,4,2048]{3,2,1,0:T(4,128)(2,1)S(1)}, bf16[2,1,4,2048]{3,2,1,0:T(4,128)(2,1)}, u32[]{:S(2)}) %copy-start.23) | copy-done | bytes 32792
  26.7 0.4 local.1
  27.1 0.6 copy-done.9
  27.8 0.6 copy-done.11
  28.4 0.0 collective-permute-done.1.refs_2_
  28.4 0.0 collective-permute-done.2.refs_3_
  28.4 0.3 collective-permute-done.6.refs_7_
  28.7 0.9 %collective-permute-done.4.refs_5_ = bf16[128,512]{1,0:T(8,128)(2,1)} collective-permute-done((bf16[128,512]{1,0:T(8,128)(2,1)}, bf16[128,512]{1,0:T(8,128)(2,1)}, u32[]{:S(2)}, u32[]{:S(2)}) %collective-permute-start.4) | collective-permute-done | bytes 131104 | tf_op jit(solution)/shard_map/ppermute | solution.py:459
  29.5 0.4 collective-permute-done.5.refs_6_
  29.9 0.0 copy-done.2
  29.9 0.0 copy-done.5
  29.9 0.0 copy-start
  30.0 2.2 %copy-done = bf16[512,4096]{1,0:T(8,128)(2,1)S(1)} copy-done((bf16[512,4096]{1,0:T(8,128)(2,1)S(1)}, bf16[512,4096]{1,0:T(8,128)(2,1)}, u32[]{:S(2)}) %copy-start) | copy-done | bytes 4194328
  32.1 2.2 %copy-done.1 = bf16[512,4096]{1,0:T(8,128)(2,1)S(1)} copy-done((bf16[512,4096]{1,0:T(8,128)(2,1)S(1)}, bf16[512,4096]{1,0:T(8,128)(2,1)}, u32[]{:S(2)}) %copy-start.1) | copy-done | bytes 4194328
  34.3 1.2 %copy-done.4 = bf16[4096,128]{1,0:T(8,128)(2,1)S(1)} copy-done((bf16[4096,128]{1,0:T(8,128)(2,1)S(1)}, bf16[4096,128]{1,0:T(8,128)(2,1)}, u32[]{:S(2)}) %copy-start.4) | copy-done | bytes 1048600
  35.5 0.9 %copy-done.7 = bf16[128,512]{1,0:T(8,128)(2,1)S(1)} copy-done((bf16[128,512]{1,0:T(8,128)(2,1)S(1)}, bf16[128,512]{1,0:T(8,128)(2,1)}, u32[]{:S(2)}) %copy-start.7) | copy-done | bytes 131096
  36.5 0.7 %copy-done.15 = f32[4096]{0:T(1024)S(1)} copy-done((f32[4096]{0:T(1024)S(1)}, f32[4096]{0:T(1024)}, u32[]{:S(2)}) %copy-start.15) | copy-done | bytes 16408
  37.2 0.7 %copy-done.17 = f32[512]{0:T(512)S(1)} copy-done((f32[512]{0:T(512)S(1)}, f32[512]{0:T(512)}, u32[]{:S(2)}) %copy-start.17) | copy-done | bytes 2072
  37.9 0.7 copy-done.18
  38.5 8.2 %factors.1 = bf16[8,32,512]{2,1,0:T(8,128)(2,1)} custom-call(f32[8,2048]{1,0:T(8,128)S(1)} %get-tuple-element.8.earlier_ref.query_ref, s32[8]{0:T(128)S(1)} %bitcast.21, bf16[128,512]{1,0:T(8,128)(2,1)S(1)} %pick.1.refs_0_, bf16[128,512]{1,0:T(8,128)(2,1)S(1)} %copy-done.7, bf16[128,512]{1,0:T(8,128)(2,1)} %collective-permute-done.1.refs_2_, ...), custom_call_target="tpu_custom_call" | custom-call | flops 1073741824 | bytes 8388608 | tf_op jit(solution)/shard_map/factors/pallas_call | solution.py:229
  46.7 4.6 %all-to-all-start = ((bf16[8,32,512]{2,1,0:T(8,128)(2,1)}), bf16[8,32,512]{2,1,0:T(8,128)(2,1)S(1)}, u32[]{:S(2)}, u32[]{:S(2)}) async-start(bf16[8,32,512]{2,1,0:T(8,128)(2,1)} %factors.1), calls=%async_computation | async-start | bytes 524288 | tf_op jit(solution)/shard_map/all_to_all | solution.py:470
  51.3 9.1 %all-to-all-done.handed_ref = bf16[8,32,512]{2,1,0:T(8,128)(2,1)S(1)} async-done(((bf16[8,32,512]{2,1,0:T(8,128)(2,1)}), bf16[8,32,512]{2,1,0:T(8,128)(2,1)S(1)}, u32[]{:S(2)}, u32[]{:S(2)}) %all-to-all-start) | async-done | bytes 262176 | tf_op jit(solution)/shard_map/all_to_all | solution.py:470
  60.4 0.1 collective-permute-start.7
  60.5 1.3 %collective-permute-done.7.other_ref = bf16[4,32,512]{2,1,0:T(8,128)(2,1)S(1)} collective-permute-done((bf16[4,32,512]{2,1,0:T(8,128)(2,1)S(1)}, bf16[4,32,512]{2,1,0:T(8,128)(2,1)S(1)}, u32[]{:S(2)}, u32[]{:S(2)}) %collective-permute-start.7) | collective-permute-done | bytes 131104 | tf_op jit(solution)/shard_map/ppermute | solution.py:473
  61.8 0.8 %copy-done.10 = f32[8,2048]{1,0:T(8,128)S(1)} copy-done((f32[8,2048]{1,0:T(8,128)S(1)}, f32[8,2048]{1,0:T(8,128)}, u32[]{:S(2)}) %copy-start.10) | copy-done | bytes 65560
  62.7 0.8 %copy-done.12 = f32[8,2048]{1,0:T(8,128)S(1)} copy-done((f32[8,2048]{1,0:T(8,128)S(1)}, f32[8,2048]{1,0:T(8,128)}, u32[]{:S(2)}) %copy-start.12) | copy-done | bytes 65560
  63.5 0.7 %copy-done.14 = f32[4096]{0:T(1024)S(1)} copy-done((f32[4096]{0:T(1024)S(1)}, f32[4096]{0:T(1024)}, u32[]{:S(2)}) %copy-start.14) | copy-done | bytes 16408
  64.2 1.6 %decode.1 = bf16[2,4,2048]{2,1,0:T(4,128)(2,1)} custom-call(bf16[8,32,512]{2,1,0:T(8,128)(2,1)S(1)} %all-to-all-done.handed_ref, bf16[4,32,512]{2,1,0:T(8,128)(2,1)S(1)} %collective-permute-done.7.other_ref, f32[8,2048]{1,0:T(8,128)S(1)} %get-tuple-element.8.earlier_ref.query_ref, f32[8,2048]{1,0:T(8,128)S(1)} %copy-done.10, f32[8,2048]{1,0:T(8,128)S(1)} %copy-done.12, ...), custom_call_target="tpu_custom_call" | custom-call | tf_op jit(solution)/shard_map/decode/pallas_call | solution.py:379
  (26 shorter events, 0.1 us)
Async XLA Ops:
  0.0 0.7 %copy-start.16 = (s32[1,8,16]{2,1,0:T(8,128)S(1)}, s32[1,8,16]{2,1,0:T(8,128)}, u32[]{:S(2)}) copy-start(s32[1,8,16]{2,1,0:T(8,128)} %param.20) | copy-start | bytes 1540
  0.7 22.1 %copy-start.24 = (f32[64,64]{1,0:T(8,128)S(1)}, f32[64,64]{1,0:T(8,128)}, u32[]{:S(2)}) copy-start(f32[64,64]{1,0:T(8,128)} %param.32) | copy-start | bytes 49156
  0.7 29.2 %copy-start.2 = (bf16[4096,192]{0,1:T(8,128)(2,1)S(1)}, bf16[4096,192]{0,1:T(8,128)(2,1)}, u32[]{:S(2)}) copy-start(bf16[4096,192]{0,1:T(8,128)(2,1)} %param.25) | copy-start | bytes 4718596
  0.7 29.2 %copy-start.3 = (bf16[3,64,4096]{2,1,0:T(8,128)(2,1)S(1)}, bf16[3,64,4096]{2,1,0:T(8,128)(2,1)}, u32[]{:S(2)}) copy-start(bf16[3,64,4096]{2,1,0:T(8,128)(2,1)} %refs_11_.1) | copy-start | bytes 4718596
  0.7 29.2 %copy-start.5 = (bf16[128,512]{1,0:T(8,128)(2,1)S(1)}, bf16[128,512]{1,0:T(8,128)(2,1)}, u32[]{:S(2)}) copy-start(bf16[128,512]{1,0:T(8,128)(2,1)} %refs_14_.1) | copy-start | bytes 393220
  0.7 29.2 %copy-start.8 = (f32[3,4096]{1,0:T(4,128)S(1)}, f32[3,4096]{1,0:T(4,128)}, u32[]{:S(2)}) copy-start(f32[3,4096]{1,0:T(4,128)} %refs_9_.1) | copy-start | bytes 147460
  9.4 10.6 %collective-permute-start.3 = (bf16[128,512]{1,0:T(8,128)(2,1)S(1)}, bf16[128,512]{1,0:T(8,128)(2,1)}, u32[]{:S(2)}, u32[]{:S(2)}) collective-permute-start(bf16[128,512]{1,0:T(8,128)(2,1)S(1)} %pick.1.refs_0_), channel_id=1, source_target_pairs={{0,8},{2,10},{4,12},{6,14},{8,0},{10,2},{12,4},{14,6},{1,9},{3,11}... | collective-permute-start | bytes 393224 | tf_op jit(solution)/shard_map/ppermute | solution.py:459
  13.5 8.6 %collective-permute-start = (bf16[128,512]{1,0:T(8,128)(2,1)S(1)}, bf16[128,512]{1,0:T(8,128)(2,1)S(1)}, u32[]{:S(2)}, u32[]{:S(2)}) collective-permute-start(bf16[128,512]{1,0:T(8,128)(2,1)S(1)} %pick.1.refs_0_), channel_id=1, source_target_pairs={{0,2},{2,0},{4,6},{6,4},{8,10},{10,8},{12,14},{14,12},{1,3},{3,1},... | collective-permute-start | bytes 393224 | tf_op jit(solution)/shard_map/ppermute | solution.py:459
  15.0 13.3 %collective-permute-start.1 = (bf16[128,512]{1,0:T(8,128)(2,1)S(1)}, bf16[128,512]{1,0:T(8,128)(2,1)}, u32[]{:S(2)}, u32[]{:S(2)}) collective-permute-start(bf16[128,512]{1,0:T(8,128)(2,1)S(1)} %pick.1.refs_0_), channel_id=1, source_target_pairs={{0,4},{2,6},{4,0},{6,2},{8,12},{10,14},{12,8},{14,10},{1,5},{3,7},... | collective-permute-start | bytes 393224 | tf_op jit(solution)/shard_map/ppermute | solution.py:459
  16.6 11.8 %collective-permute-start.2 = (bf16[128,512]{1,0:T(8,128)(2,1)S(1)}, bf16[128,512]{1,0:T(8,128)(2,1)}, u32[]{:S(2)}, u32[]{:S(2)}) collective-permute-start(bf16[128,512]{1,0:T(8,128)(2,1)S(1)} %pick.1.refs_0_), channel_id=1, source_target_pairs={{0,6},{2,4},{4,2},{6,0},{8,14},{10,12},{12,10},{14,8},{1,7},{3,5},... | collective-permute-start | bytes 393224 | tf_op jit(solution)/shard_map/ppermute | solution.py:459
  17.0 11.7 %collective-permute-start.6 = (bf16[128,512]{1,0:T(8,128)(2,1)S(1)}, bf16[128,512]{1,0:T(8,128)(2,1)}, u32[]{:S(2)}, u32[]{:S(2)}) collective-permute-start(bf16[128,512]{1,0:T(8,128)(2,1)S(1)} %pick.1.refs_0_), channel_id=1, source_target_pairs={{0,14},{2,12},{4,10},{6,8},{8,6},{10,4},{12,2},{14,0},{1,15},{3,13... | collective-permute-start | bytes 393224 | tf_op jit(solution)/shard_map/ppermute | solution.py:459
  20.0 9.5 %collective-permute-start.4 = (bf16[128,512]{1,0:T(8,128)(2,1)}, bf16[128,512]{1,0:T(8,128)(2,1)}, u32[]{:S(2)}, u32[]{:S(2)}) collective-permute-start(bf16[128,512]{1,0:T(8,128)(2,1)} %collective-permute-done.3.refs_4_), channel_id=1, source_target_pairs={{0,2},{2,0},{4,6},{6,4},{8,10},{10,8},{12,14},{14,12},{1,3},{3,1},... | collective-permute-start | bytes 393224 | tf_op jit(solution)/shard_map/ppermute | solution.py:459
  22.1 0.6 copy-start.6
  22.7 7.2 %collective-permute-start.5 = (bf16[128,512]{1,0:T(8,128)(2,1)}, bf16[128,512]{1,0:T(8,128)(2,1)}, u32[]{:S(2)}, u32[]{:S(2)}) collective-permute-start(bf16[128,512]{1,0:T(8,128)(2,1)} %collective-permute-done.3.refs_4_), channel_id=1, source_target_pairs={{0,4},{2,6},{4,0},{6,2},{8,12},{10,14},{12,8},{14,10},{1,5},{3,7},... | collective-permute-start | bytes 393224 | tf_op jit(solution)/shard_map/ppermute | solution.py:459
  22.9 0.8 %copy-start.19 = (bf16[2,1,4,2048]{3,2,1,0:T(4,128)(2,1)S(1)}, bf16[2,1,4,2048]{3,2,1,0:T(4,128)(2,1)}, u32[]{:S(2)}) copy-start(bf16[2,1,4,2048]{3,2,1,0:T(4,128)(2,1)} %param.35) | copy-start | bytes 98308
  23.7 0.8 %copy-start.20 = (bf16[2,1,4,2048]{3,2,1,0:T(4,128)(2,1)S(1)}, bf16[2,1,4,2048]{3,2,1,0:T(4,128)(2,1)}, u32[]{:S(2)}) copy-start(bf16[2,1,4,2048]{3,2,1,0:T(4,128)(2,1)} %param.36) | copy-start | bytes 98308
  24.4 0.8 %copy-start.21 = (bf16[2,1,4,2048]{3,2,1,0:T(4,128)(2,1)S(1)}, bf16[2,1,4,2048]{3,2,1,0:T(4,128)(2,1)}, u32[]{:S(2)}) copy-start(bf16[2,1,4,2048]{3,2,1,0:T(4,128)(2,1)} %param.37) | copy-start | bytes 98308
  25.2 0.8 %copy-start.22 = (bf16[2,1,4,2048]{3,2,1,0:T(4,128)(2,1)S(1)}, bf16[2,1,4,2048]{3,2,1,0:T(4,128)(2,1)}, u32[]{:S(2)}) copy-start(bf16[2,1,4,2048]{3,2,1,0:T(4,128)(2,1)} %param.38) | copy-start | bytes 98308
  26.0 0.8 %copy-start.23 = (bf16[2,1,4,2048]{3,2,1,0:T(4,128)(2,1)S(1)}, bf16[2,1,4,2048]{3,2,1,0:T(4,128)(2,1)}, u32[]{:S(2)}) copy-start(bf16[2,1,4,2048]{3,2,1,0:T(4,128)(2,1)} %param.39) | copy-start | bytes 98308
  27.1 0.6 copy-start.9
  27.8 0.6 copy-start.11
  29.9 2.2 %copy-start = (bf16[512,4096]{1,0:T(8,128)(2,1)S(1)}, bf16[512,4096]{1,0:T(8,128)(2,1)}, u32[]{:S(2)}) copy-start(bf16[512,4096]{1,0:T(8,128)(2,1)} %refs_15_.1) | copy-start | bytes 12582916
  32.1 2.2 %copy-start.1 = (bf16[512,4096]{1,0:T(8,128)(2,1)S(1)}, bf16[512,4096]{1,0:T(8,128)(2,1)}, u32[]{:S(2)}) copy-start(bf16[512,4096]{1,0:T(8,128)(2,1)} %refs_16_.1) | copy-start | bytes 12582916
  34.3 1.2 %copy-start.4 = (bf16[4096,128]{1,0:T(8,128)(2,1)S(1)}, bf16[4096,128]{1,0:T(8,128)(2,1)}, u32[]{:S(2)}) copy-start(bf16[4096,128]{1,0:T(8,128)(2,1)} %refs_13_.1) | copy-start | bytes 3145732
  35.5 0.9 %copy-start.7 = (bf16[128,512]{1,0:T(8,128)(2,1)S(1)}, bf16[128,512]{1,0:T(8,128)(2,1)}, u32[]{:S(2)}) copy-start(bf16[128,512]{1,0:T(8,128)(2,1)} %copy-done.6) | copy-start | bytes 393220
  36.5 0.7 %copy-start.15 = (f32[4096]{0:T(1024)S(1)}, f32[4096]{0:T(1024)}, u32[]{:S(2)}) copy-start(f32[4096]{0:T(1024)} %param.23) | copy-start | bytes 49156
  37.2 0.7 %copy-start.17 = (f32[512]{0:T(512)S(1)}, f32[512]{0:T(512)}, u32[]{:S(2)}) copy-start(f32[512]{0:T(512)} %param.27) | copy-start | bytes 6148
  37.9 0.7 copy-start.18
  38.5 23.3 %copy-start.13 = (f32[4096]{0:T(1024)S(1)}, f32[4096]{0:T(1024)}, u32[]{:S(2)}) copy-start(f32[4096]{0:T(1024)} %param.33) | copy-start | bytes 49156
  46.7 13.7 %all-to-all-start = ((bf16[8,32,512]{2,1,0:T(8,128)(2,1)}), bf16[8,32,512]{2,1,0:T(8,128)(2,1)S(1)}, u32[]{:S(2)}, u32[]{:S(2)}) async-start(bf16[8,32,512]{2,1,0:T(8,128)(2,1)} %factors.1), calls=%async_computation | async-start | bytes 524288 | tf_op jit(solution)/shard_map/all_to_all | solution.py:470
  60.4 1.4 %collective-permute-start.7 = (bf16[4,32,512]{2,1,0:T(8,128)(2,1)S(1)}, bf16[4,32,512]{2,1,0:T(8,128)(2,1)S(1)}, u32[]{:S(2)}, u32[]{:S(2)}) collective-permute-start(bf16[4,32,512]{2,1,0:T(8,128)(2,1)S(1)} %constant_dynamic-slice_fusion), channel_id=1, source_target_pairs={{0,1},{1,0},{2,3},{3,2},{4,5},{5,4},{6,7},{7,6},{8,9},{9,8},{10,11... | collective-permute-start | bytes 393224 | tf_op jit(solution)/shard_map/ppermute | solution.py:473
  61.8 0.8 %copy-start.10 = (f32[8,2048]{1,0:T(8,128)S(1)}, f32[8,2048]{1,0:T(8,128)}, u32[]{:S(2)}) copy-start(f32[8,2048]{1,0:T(8,128)} %copy-done.9) | copy-start | bytes 196612
  62.7 0.8 %copy-start.12 = (f32[8,2048]{1,0:T(8,128)S(1)}, f32[8,2048]{1,0:T(8,128)}, u32[]{:S(2)}) copy-start(f32[8,2048]{1,0:T(8,128)} %copy-done.11) | copy-start | bytes 196612
  63.5 0.7 %copy-start.14 = (f32[4096]{0:T(1024)S(1)}, f32[4096]{0:T(1024)}, u32[]{:S(2)}) copy-start(f32[4096]{0:T(1024)} %param.34) | copy-start | bytes 49156

commit v3 on v2

--- a/solution.py
+++ b/solution.py
@@ -100,7 +100,7 @@
     )(ids, table)
 
 
-def factor_kernel(earlier_ref, spans_ref, *refs, offsets, single, width, length, rank):
+def factor_kernel(spans_ref, *refs, offsets, single, width, length, rank):
     blocks = len(offsets)
     place = lax.axis_index("wide") if blocks > 1 else 0
     embeds = refs[:blocks]
@@ -179,7 +179,6 @@
 
 
 def factors(
-    earlier,
     embeds,
     offsets,
     lengths,
@@ -214,13 +213,13 @@
     )
     out = jax.ShapeDtypeStruct((tokens // length, 2 * length, columns), bf16)
     if single:
-        places = dict(in_specs=[ANY, SMEM] + [VMEM] * (len(embeds) + len(weights)), out_specs=VMEM)
+        places = dict(in_specs=[SMEM] + [VMEM] * (len(embeds) + len(weights)), out_specs=VMEM)
         limit = 20 << 20
     else:
         kept = [pl.BlockSpec(x.shape, lambda i, rank=x.ndim: (0,) * rank) for x in weights]
         places = dict(
             grid=(tokens // rows,),
-            in_specs=[ANY, SMEM]
+            in_specs=[SMEM]
             + [pl.BlockSpec((rows, block_width), lambda i: (i, 0)) for _ in embeds]
             + kept,
             out_specs=pl.BlockSpec((rows // length,) + out.shape[1:], lambda i: (i, 0, 0)),
@@ -240,7 +239,7 @@
         compiler_params=pltpu.CompilerParams(vmem_limit_bytes=limit),
         name="factors",
         **places,
-    )(earlier, lengths, *embeds, *weights)
+    )(lengths, *embeds, *weights)
 
 
 def head_ones(wide, head):
@@ -441,7 +440,8 @@
             generated_valve_scores,
         )
     ]
-    picked = pick(symbol_vector_lookup, context_symbol_ids[0])
+    ids = pltpu.with_memory_space_constraint(context_symbol_ids[0], pltpu.HBM)
+    picked = pick(symbol_vector_lookup, ids)
     weights = (
         opening_lagged_blend,
         lagged_blend_weights,
@@ -466,7 +466,7 @@
         embeds = [gathered.transpose(1, 0, 2).reshape(picked.shape[0], wide * columns)]
         offsets = (0,)
     prepared = local(streams, present_symbol_reward.reshape(1, -1), head)
-    parcel = factors(prepared[0], embeds, offsets, lengths, length, *weights)
+    parcel = factors(embeds, offsets, lengths, length, *weights)
     handed = lax.all_to_all(parcel, "wide", split_axis=0, concat_axis=0, tiled=True)
     share = wide // narrow
     away = lax.dynamic_slice_in_dim(handed, (1 - core) * share, share, 0)

time: 66.9 us -> 54.3 us (0.81); the launches traced: 65.9 us -> 54.1 us
  local copies, waits for them, and re-layouts: 17.4 us -> 0.19 us
  waiting for transfers between devices: 12.7 us -> 18.1 us
    unnamed x50 -> x36, local copies, waits for them, and re-layouts: 17.3 us -> 0.09 us
    ppermute x7, waiting for transfers between devices: 2.27 us -> 8.23 us  [per_device(): lax.ppermute(held[source], 'wide', [(i, i ^ hop) for i in range(wide)])]
  transfers between devices with their start and end apart: 9 -> 9, of which waited for: 6 -> 8; matrix products, arithmetic and copies ran while one was open for 0% -> 0% of each run, Pallas kernels for 1% -> 1%
where the time goes in v3:
time: 54.3 us; the launch traced here: 54.1 us
  Pallas kernels  18.6 us (34%)
  waiting for transfers between devices  18.1 us (33%)
  starting transfers between devices  16.9 us (31%)
    ppermute x7, starting transfers between devices, per_device(): lax.ppermute(held[source], 'wide', [(i, i ^ hop) for i in range(wide)])  12.2 us
    all_to_all x1, waiting for transfers between devices, per_device(): lax.all_to_all(parcel, 'wide', split_axis=0, concat_axis=0, tiled=True)  9.1 us
    pallas_call x1, Pallas kernels, pick(): pl.pallas_call(functools.partial(pick_kernel, batch=batch, ahead=4), out_...  9.04 us
    ppermute x7, waiting for transfers between devices, per_device(): lax.ppermute(held[source], 'wide', [(i, i ^ hop) for i in range(wide)])  8.23 us
    pallas_call x1, Pallas kernels, factors(): pl.pallas_call(functools.partial(factor_kernel, offsets=offsets, single=s...  7.53 us
    all_to_all x1, starting transfers between devices, per_device(): lax.all_to_all(parcel, 'wide', split_axis=0, concat_axis=0, tiled=True)  4.63 us
    pallas_call x1, Pallas kernels, decode(): pl.pallas_call(functools.partial(decode_kernel, head=head, length=length)...  1.65 us
  transfers between devices with their start and end apart: 9, of which 8 were waited for; matrix products, arithmetic and copies ran while one was open for 0% of the time, Pallas kernels for 1%

profile of v3, /device:TPU:0, one launch (start us, length us, event | category | flops | bytes accessed | tf_op | source)
XLA Modules:
  0.0 54.1 jit_solution(11887196138815078491)
XLA Ops:
  0.0 0.0 copy-start.5
  0.0 0.0 copy-start.6
  0.0 0.0 copy-start.9
  0.0 0.0 copy-start.10
  0.1 0.0 copy-start.11
  0.1 9.0 %pick.1.refs_0_ = bf16[128,512]{1,0:T(8,128)(2,1)S(1)} custom-call(s32[8,16]{1,0:T(8,128)} %bitcast.26, bf16[512,32768]{1,0:T(8,128)(2,1)} %table_ref.1), custom_call_target="tpu_custom_call" | custom-call | bytes 16777216 | tf_op jit(solution)/shard_map/pick/pallas_call | solution.py:87
  9.1 4.2 %collective-permute-start.3 = (bf16[128,512]{1,0:T(8,128)(2,1)S(1)}, bf16[128,512]{1,0:T(8,128)(2,1)S(1)}, u32[]{:S(2)}, u32[]{:S(2)}) collective-permute-start(bf16[128,512]{1,0:T(8,128)(2,1)S(1)} %pick.1.refs_0_), channel_id=1, source_target_pairs={{0,8},{2,10},{4,12},{6,14},{8,0},{10,2},{12,4},{14,6},{1,9},{3,11}... | collective-permute-start | bytes 393224 | tf_op jit(solution)/shard_map/ppermute | solution.py:459
  13.3 1.5 %collective-permute-start = (bf16[128,512]{1,0:T(8,128)(2,1)S(1)}, bf16[128,512]{1,0:T(8,128)(2,1)S(1)}, u32[]{:S(2)}, u32[]{:S(2)}) collective-permute-start(bf16[128,512]{1,0:T(8,128)(2,1)S(1)} %pick.1.refs_0_), channel_id=1, source_target_pairs={{0,2},{2,0},{4,6},{6,4},{8,10},{10,8},{12,14},{14,12},{1,3},{3,1},... | collective-permute-start | bytes 393224 | tf_op jit(solution)/shard_map/ppermute | solution.py:459
  14.8 1.6 %collective-permute-start.1 = (bf16[128,512]{1,0:T(8,128)(2,1)S(1)}, bf16[128,512]{1,0:T(8,128)(2,1)S(1)}, u32[]{:S(2)}, u32[]{:S(2)}) collective-permute-start(bf16[128,512]{1,0:T(8,128)(2,1)S(1)} %pick.1.refs_0_), channel_id=1, source_target_pairs={{0,4},{2,6},{4,0},{6,2},{8,12},{10,14},{12,8},{14,10},{1,5},{3,7},... | collective-permute-start | bytes 393224 | tf_op jit(solution)/shard_map/ppermute | solution.py:459
  16.4 0.4 collective-permute-start.2
  16.8 2.3 %collective-permute-start.6 = (bf16[128,512]{1,0:T(8,128)(2,1)S(1)}, bf16[128,512]{1,0:T(8,128)(2,1)S(1)}, u32[]{:S(2)}, u32[]{:S(2)}) collective-permute-start(bf16[128,512]{1,0:T(8,128)(2,1)S(1)} %pick.1.refs_0_), channel_id=1, source_target_pairs={{0,14},{2,12},{4,10},{6,8},{8,6},{10,4},{12,2},{14,0},{1,15},{3,13... | collective-permute-start | bytes 393224 | tf_op jit(solution)/shard_map/ppermute | solution.py:459
  19.1 0.6 %collective-permute-done.3.refs_4_ = bf16[128,512]{1,0:T(8,128)(2,1)S(1)} collective-permute-done((bf16[128,512]{1,0:T(8,128)(2,1)S(1)}, bf16[128,512]{1,0:T(8,128)(2,1)S(1)}, u32[]{:S(2)}, u32[]{:S(2)}) %collective-permute-start.3) | collective-permute-done | bytes 131104 | tf_op jit(solution)/shard_map/ppermute | solution.py:459
  19.7 2.1 %collective-permute-start.4 = (bf16[128,512]{1,0:T(8,128)(2,1)S(1)}, bf16[128,512]{1,0:T(8,128)(2,1)S(1)}, u32[]{:S(2)}, u32[]{:S(2)}) collective-permute-start(bf16[128,512]{1,0:T(8,128)(2,1)S(1)} %collective-permute-done.3.refs_4_), channel_id=1, source_target_pairs={{0,2},{2,0},{4,6},{6,4},{8,10},{10,8},{12,14},{14,12},{1,3},{3,1},... | collective-permute-start | bytes 393224 | tf_op jit(solution)/shard_map/ppermute | solution.py:459
  21.7 0.0 collective-permute-done.refs_1_
  21.7 0.2 collective-permute-start.5
  22.0 0.1 collective-permute-done.1.refs_2_
  22.1 5.4 %collective-permute-done.2.refs_3_ = bf16[128,512]{1,0:T(8,128)(2,1)S(1)} collective-permute-done((bf16[128,512]{1,0:T(8,128)(2,1)S(1)}, bf16[128,512]{1,0:T(8,128)(2,1)S(1)}, u32[]{:S(2)}, u32[]{:S(2)}) %collective-permute-start.2) | collective-permute-done | bytes 131104 | tf_op jit(solution)/shard_map/ppermute | solution.py:459
  27.5 0.9 %collective-permute-done.6.refs_7_ = bf16[128,512]{1,0:T(8,128)(2,1)S(1)} collective-permute-done((bf16[128,512]{1,0:T(8,128)(2,1)S(1)}, bf16[128,512]{1,0:T(8,128)(2,1)S(1)}, u32[]{:S(2)}, u32[]{:S(2)}) %collective-permute-start.6) | collective-permute-done | bytes 131104 | tf_op jit(solution)/shard_map/ppermute | solution.py:459
  28.3 0.7 %collective-permute-done.4.refs_5_ = bf16[128,512]{1,0:T(8,128)(2,1)S(1)} collective-permute-done((bf16[128,512]{1,0:T(8,128)(2,1)S(1)}, bf16[128,512]{1,0:T(8,128)(2,1)S(1)}, u32[]{:S(2)}, u32[]{:S(2)}) %collective-permute-start.4) | collective-permute-done | bytes 131104 | tf_op jit(solution)/shard_map/ppermute | solution.py:459
  29.0 0.5 %collective-permute-done.5.refs_6_ = bf16[128,512]{1,0:T(8,128)(2,1)S(1)} collective-permute-done((bf16[128,512]{1,0:T(8,128)(2,1)S(1)}, bf16[128,512]{1,0:T(8,128)(2,1)S(1)}, u32[]{:S(2)}, u32[]{:S(2)}) %collective-permute-start.5) | collective-permute-done | bytes 131104 | tf_op jit(solution)/shard_map/ppermute | solution.py:459
  29.6 0.0 copy-done
  29.6 0.0 copy-done.1
  29.6 0.0 copy-done.2
  29.6 0.0 copy-done.3
  29.6 0.0 copy-done.4
  29.6 0.0 copy-done.5
  29.6 0.0 copy-done.6
  29.6 0.0 copy-done.9
  29.6 0.0 copy-done.10
  29.6 0.0 copy-done.11
  29.7 0.0 copy-start.17
  29.7 0.0 copy-start.12
  29.7 0.0 copy-start.13
  29.7 0.0 copy-start.14
  29.7 0.0 copy-start.15
  29.7 0.0 copy-start.16
  29.7 0.0 copy-start.7
  29.7 0.0 copy-start.8
  29.8 7.5 %factors.1 = bf16[8,32,512]{2,1,0:T(8,128)(2,1)} custom-call(s32[8]{0:T(128)S(1)} %bitcast.20, bf16[128,512]{1,0:T(8,128)(2,1)S(1)} %pick.1.refs_0_, bf16[128,512]{1,0:T(8,128)(2,1)S(1)} %collective-permute-done.refs_1_, bf16[128,512]{1,0:T(8,128)(2,1)S(1)} %collective-permute-done.1.refs_2_, bf16[128,512]{1,0:T(8,128)(2,1)S(1)} %collective-permute-done.2.refs_3_, ...), custom_call_target="tpu_custom_call" | custom-call | flops 1073741824 | bytes 8388608 | tf_op jit(solution)/shard_map/factors/pallas_call | solution.py:228
  37.3 4.6 %all-to-all-start = ((bf16[8,32,512]{2,1,0:T(8,128)(2,1)}), bf16[8,32,512]{2,1,0:T(8,128)(2,1)S(1)}, u32[]{:S(2)}, u32[]{:S(2)}) async-start(bf16[8,32,512]{2,1,0:T(8,128)(2,1)} %factors.1), calls=%async_computation | async-start | bytes 524288 | tf_op jit(solution)/shard_map/all_to_all | solution.py:470
  41.9 9.1 %all-to-all-done.handed_ref = bf16[8,32,512]{2,1,0:T(8,128)(2,1)S(1)} async-done(((bf16[8,32,512]{2,1,0:T(8,128)(2,1)}), bf16[8,32,512]{2,1,0:T(8,128)(2,1)S(1)}, u32[]{:S(2)}, u32[]{:S(2)}) %all-to-all-start) | async-done | bytes 262176 | tf_op jit(solution)/shard_map/all_to_all | solution.py:470
  51.0 0.1 collective-permute-start.7
  51.1 0.0 copy-done.17
  51.1 0.1 reshape.44.reward_ref
  51.3 0.4 local.1
  51.7 0.8 %collective-permute-done.7.other_ref = bf16[4,32,512]{2,1,0:T(8,128)(2,1)S(1)} collective-permute-done((bf16[4,32,512]{2,1,0:T(8,128)(2,1)S(1)}, bf16[4,32,512]{2,1,0:T(8,128)(2,1)S(1)}, u32[]{:S(2)}, u32[]{:S(2)}) %collective-permute-start.7) | collective-permute-done | bytes 131104 | tf_op jit(solution)/shard_map/ppermute | solution.py:473
  52.5 0.0 copy-done.8
  52.5 1.7 %decode.1 = bf16[2,4,2048]{2,1,0:T(4,128)(2,1)} custom-call(bf16[8,32,512]{2,1,0:T(8,128)(2,1)S(1)} %all-to-all-done.handed_ref, bf16[4,32,512]{2,1,0:T(8,128)(2,1)S(1)} %collective-permute-done.7.other_ref, f32[8,2048]{1,0:T(8,128)S(1)} %get-tuple-element.8.query_ref, f32[8,2048]{1,0:T(8,128)S(1)} %get-tuple-element.9.near_ref, ...), custom_call_target="tpu_custom_call" | custom-call | tf_op jit(solution)/shard_map/decode/pallas_call | solution.py:378
  (12 shorter events, 0.0 us)
Async XLA Ops:
  0.0 29.6 %copy-start = (bf16[512,4096]{1,0:T(8,128)(2,1)S(1)}, bf16[512,4096]{1,0:T(8,128)(2,1)}, u32[]{:S(2)}) copy-start(bf16[512,4096]{1,0:T(8,128)(2,1)} %refs_15_.1) | copy-start | bytes 12582916
  0.0 29.6 %copy-start.1 = (bf16[512,4096]{1,0:T(8,128)(2,1)S(1)}, bf16[512,4096]{1,0:T(8,128)(2,1)}, u32[]{:S(2)}) copy-start(bf16[512,4096]{1,0:T(8,128)(2,1)} %refs_16_.1) | copy-start | bytes 12582916
  0.0 29.6 %copy-start.2 = (bf16[4096,192]{0,1:T(8,128)(2,1)S(1)}, bf16[4096,192]{0,1:T(8,128)(2,1)}, u32[]{:S(2)}) copy-start(bf16[4096,192]{0,1:T(8,128)(2,1)} %param.25) | copy-start | bytes 4718596
  0.0 29.6 %copy-start.3 = (bf16[3,64,4096]{2,1,0:T(8,128)(2,1)S(1)}, bf16[3,64,4096]{2,1,0:T(8,128)(2,1)}, u32[]{:S(2)}) copy-start(bf16[3,64,4096]{2,1,0:T(8,128)(2,1)} %refs_11_.1) | copy-start | bytes 4718596
  0.0 29.6 %copy-start.4 = (bf16[4096,128]{1,0:T(8,128)(2,1)S(1)}, bf16[4096,128]{1,0:T(8,128)(2,1)}, u32[]{:S(2)}) copy-start(bf16[4096,128]{1,0:T(8,128)(2,1)} %refs_13_.1) | copy-start | bytes 3145732
  0.0 29.6 %copy-start.5 = (bf16[128,512]{1,0:T(8,128)(2,1)S(1)}, bf16[128,512]{1,0:T(8,128)(2,1)}, u32[]{:S(2)}) copy-start(bf16[128,512]{1,0:T(8,128)(2,1)} %refs_14_.1) | copy-start | bytes 393220
  0.0 29.6 %copy-start.6 = (f32[3,4096]{1,0:T(4,128)S(1)}, f32[3,4096]{1,0:T(4,128)}, u32[]{:S(2)}) copy-start(f32[3,4096]{1,0:T(4,128)} %refs_9_.1) | copy-start | bytes 147460
  0.0 29.6 %copy-start.9 = (f32[4096]{0:T(1024)S(1)}, f32[4096]{0:T(1024)}, u32[]{:S(2)}) copy-start(f32[4096]{0:T(1024)} %param.23) | copy-start | bytes 49156
  0.0 29.6 %copy-start.10 = (f32[512]{0:T(512)S(1)}, f32[512]{0:T(512)}, u32[]{:S(2)}) copy-start(f32[512]{0:T(512)} %param.27) | copy-start | bytes 6148
  0.1 29.6 %copy-start.11 = (s32[1,8]{1,0:T(1,128)S(1)}, s32[1,8]{1,0:T(1,128)}, u32[]{:S(2)}) copy-start(s32[1,8]{1,0:T(1,128)} %param.21) | copy-start | bytes 100
  9.1 10.6 %collective-permute-start.3 = (bf16[128,512]{1,0:T(8,128)(2,1)S(1)}, bf16[128,512]{1,0:T(8,128)(2,1)S(1)}, u32[]{:S(2)}, u32[]{:S(2)}) collective-permute-start(bf16[128,512]{1,0:T(8,128)(2,1)S(1)} %pick.1.refs_0_), channel_id=1, source_target_pairs={{0,8},{2,10},{4,12},{6,14},{8,0},{10,2},{12,4},{14,6},{1,9},{3,11}... | collective-permute-start | bytes 393224 | tf_op jit(solution)/shard_map/ppermute | solution.py:459
  13.3 8.5 %collective-permute-start = (bf16[128,512]{1,0:T(8,128)(2,1)S(1)}, bf16[128,512]{1,0:T(8,128)(2,1)S(1)}, u32[]{:S(2)}, u32[]{:S(2)}) collective-permute-start(bf16[128,512]{1,0:T(8,128)(2,1)S(1)} %pick.1.refs_0_), channel_id=1, source_target_pairs={{0,2},{2,0},{4,6},{6,4},{8,10},{10,8},{12,14},{14,12},{1,3},{3,1},... | collective-permute-start | bytes 393224 | tf_op jit(solution)/shard_map/ppermute | solution.py:459
  14.8 7.3 %collective-permute-start.1 = (bf16[128,512]{1,0:T(8,128)(2,1)S(1)}, bf16[128,512]{1,0:T(8,128)(2,1)S(1)}, u32[]{:S(2)}, u32[]{:S(2)}) collective-permute-start(bf16[128,512]{1,0:T(8,128)(2,1)S(1)} %pick.1.refs_0_), channel_id=1, source_target_pairs={{0,4},{2,6},{4,0},{6,2},{8,12},{10,14},{12,8},{14,10},{1,5},{3,7},... | collective-permute-start | bytes 393224 | tf_op jit(solution)/shard_map/ppermute | solution.py:459
  16.4 11.1 %collective-permute-start.2 = (bf16[128,512]{1,0:T(8,128)(2,1)S(1)}, bf16[128,512]{1,0:T(8,128)(2,1)S(1)}, u32[]{:S(2)}, u32[]{:S(2)}) collective-permute-start(bf16[128,512]{1,0:T(8,128)(2,1)S(1)} %pick.1.refs_0_), channel_id=1, source_target_pairs={{0,6},{2,4},{4,2},{6,0},{8,14},{10,12},{12,10},{14,8},{1,7},{3,5},... | collective-permute-start | bytes 393224 | tf_op jit(solution)/shard_map/ppermute | solution.py:459
  16.8 11.6 %collective-permute-start.6 = (bf16[128,512]{1,0:T(8,128)(2,1)S(1)}, bf16[128,512]{1,0:T(8,128)(2,1)S(1)}, u32[]{:S(2)}, u32[]{:S(2)}) collective-permute-start(bf16[128,512]{1,0:T(8,128)(2,1)S(1)} %pick.1.refs_0_), channel_id=1, source_target_pairs={{0,14},{2,12},{4,10},{6,8},{8,6},{10,4},{12,2},{14,0},{1,15},{3,13... | collective-permute-start | bytes 393224 | tf_op jit(solution)/shard_map/ppermute | solution.py:459
  19.7 9.4 %collective-permute-start.4 = (bf16[128,512]{1,0:T(8,128)(2,1)S(1)}, bf16[128,512]{1,0:T(8,128)(2,1)S(1)}, u32[]{:S(2)}, u32[]{:S(2)}) collective-permute-start(bf16[128,512]{1,0:T(8,128)(2,1)S(1)} %collective-permute-done.3.refs_4_), channel_id=1, source_target_pairs={{0,2},{2,0},{4,6},{6,4},{8,10},{10,8},{12,14},{14,12},{1,3},{3,1},... | collective-permute-start | bytes 393224 | tf_op jit(solution)/shard_map/ppermute | solution.py:459
  21.7 7.8 %collective-permute-start.5 = (bf16[128,512]{1,0:T(8,128)(2,1)S(1)}, bf16[128,512]{1,0:T(8,128)(2,1)S(1)}, u32[]{:S(2)}, u32[]{:S(2)}) collective-permute-start(bf16[128,512]{1,0:T(8,128)(2,1)S(1)} %collective-permute-done.3.refs_4_), channel_id=1, source_target_pairs={{0,4},{2,6},{4,0},{6,2},{8,12},{10,14},{12,8},{14,10},{1,5},{3,7},... | collective-permute-start | bytes 393224 | tf_op jit(solution)/shard_map/ppermute | solution.py:459
  29.7 21.5 %copy-start.17 = (f32[64,64]{1,0:T(8,128)S(1)}, f32[64,64]{1,0:T(8,128)}, u32[]{:S(2)}) copy-start(f32[64,64]{1,0:T(8,128)} %param.32) | copy-start | bytes 49156
  29.7 21.5 %copy-start.12 = (bf16[2,1,4,2048]{3,2,1,0:T(4,128)(2,1)S(1)}, bf16[2,1,4,2048]{3,2,1,0:T(4,128)(2,1)}, u32[]{:S(2)}) copy-start(bf16[2,1,4,2048]{3,2,1,0:T(4,128)(2,1)} %param.35) | copy-start | bytes 98308
  29.7 21.5 %copy-start.13 = (bf16[2,1,4,2048]{3,2,1,0:T(4,128)(2,1)S(1)}, bf16[2,1,4,2048]{3,2,1,0:T(4,128)(2,1)}, u32[]{:S(2)}) copy-start(bf16[2,1,4,2048]{3,2,1,0:T(4,128)(2,1)} %param.36) | copy-start | bytes 98308
  29.7 21.5 %copy-start.14 = (bf16[2,1,4,2048]{3,2,1,0:T(4,128)(2,1)S(1)}, bf16[2,1,4,2048]{3,2,1,0:T(4,128)(2,1)}, u32[]{:S(2)}) copy-start(bf16[2,1,4,2048]{3,2,1,0:T(4,128)(2,1)} %param.37) | copy-start | bytes 98308
  29.7 21.5 %copy-start.15 = (bf16[2,1,4,2048]{3,2,1,0:T(4,128)(2,1)S(1)}, bf16[2,1,4,2048]{3,2,1,0:T(4,128)(2,1)}, u32[]{:S(2)}) copy-start(bf16[2,1,4,2048]{3,2,1,0:T(4,128)(2,1)} %param.38) | copy-start | bytes 98308
  29.7 21.5 %copy-start.16 = (bf16[2,1,4,2048]{3,2,1,0:T(4,128)(2,1)S(1)}, bf16[2,1,4,2048]{3,2,1,0:T(4,128)(2,1)}, u32[]{:S(2)}) copy-start(bf16[2,1,4,2048]{3,2,1,0:T(4,128)(2,1)} %param.39) | copy-start | bytes 98308
  29.7 22.7 %copy-start.7 = (f32[4096]{0:T(1024)S(1)}, f32[4096]{0:T(1024)}, u32[]{:S(2)}) copy-start(f32[4096]{0:T(1024)} %param.33) | copy-start | bytes 49156
  29.7 22.7 %copy-start.8 = (f32[4096]{0:T(1024)S(1)}, f32[4096]{0:T(1024)}, u32[]{:S(2)}) copy-start(f32[4096]{0:T(1024)} %param.34) | copy-start | bytes 49156
  37.3 13.7 %all-to-all-start = ((bf16[8,32,512]{2,1,0:T(8,128)(2,1)}), bf16[8,32,512]{2,1,0:T(8,128)(2,1)S(1)}, u32[]{:S(2)}, u32[]{:S(2)}) async-start(bf16[8,32,512]{2,1,0:T(8,128)(2,1)} %factors.1), calls=%async_computation | async-start | bytes 524288 | tf_op jit(solution)/shard_map/all_to_all | solution.py:470
  51.0 1.4 %collective-permute-start.7 = (bf16[4,32,512]{2,1,0:T(8,128)(2,1)S(1)}, bf16[4,32,512]{2,1,0:T(8,128)(2,1)S(1)}, u32[]{:S(2)}, u32[]{:S(2)}) collective-permute-start(bf16[4,32,512]{2,1,0:T(8,128)(2,1)S(1)} %constant_dynamic-slice_fusion), channel_id=1, source_target_pairs={{0,1},{1,0},{2,3},{3,2},{4,5},{5,4},{6,7},{7,6},{8,9},{9,8},{10,11... | collective-permute-start | bytes 393224 | tf_op jit(solution)/shard_map/ppermute | solution.py:473
